TPU v7x, 128 devices: a whole 4x4x4 slice. The times are simulated.
128 devices in a mesh: ex: 32 (over y, x, core), feat: 4 (over z).
Axes of the slice: x: 4, y: 4, z: 4, core: 2. Of those that a mesh axis runs over, the one named last changes fastest.
Arguments:
- features: bfloat16 [65536, 2048], P('ex', 'feat'), may hold values from -0.125 to 0.125
- weights: float32 [2048], P('feat'), may hold values from -6 to 6
- labels: int32 [65536], P('ex'), may hold values 0 or 1
- signs: int32 [65536], P('ex'), may hold values from -1 to 1, as said below
- samples: int32 [2048], replicated, may hold values from 0 to 65535
- radius: float32 [1], replicated, may hold values from 0.1 to 0.25
Outputs:
- new_weights: float32 [2048], P('feat')
Inputs may be any that keep to these rules, and one draw needn't show every extreme that they name: `signs`: each entry is -1 or +1.
All inputs are finite; a program needn't handle non-finite values. No bound on the sum of `labels` on one device may be relied on, other than what follows from the above.
Results may differ from a plain program's by a relative error of at most 0.00067.
Values may be sent and summed in bfloat16 or wider, within the bound.
A program may use at most 192 MiB of HBM per device.

v0:
```python
import math

import jax
import jax.numpy as jnp
from jax import lax
from jax.sharding import PartitionSpec as P

D = 2048
ITERS = 4


REG = 0.02


def from_partner(value, axis, bit):
    mask = 2**bit
    pairs = [(source, source ^ mask) for source in range(lax.axis_size(axis))]
    return lax.ppermute(value, axis, pairs)


def parity_bits(common, bit_total):
    parity = jnp.zeros(common.shape, jnp.int32)
    for bit_number in range(bit_total):
        parity = parity ^ common >> bit_number & 1
    return parity


def sign_table(length):
    indices = lax.iota(jnp.int32, length)
    parity = parity_bits(indices[:, None] & indices[None, :], max(1, length.bit_length()))
    return 1 - 2 * parity


def local_mix(signed):
    row_count, feat_width = signed.shape
    levels = row_count.bit_length() - 1
    outer = 2 ** (levels // 2)
    inner = row_count // outer
    shaped = signed.reshape(outer, inner, feat_width)
    first = jnp.einsum(
        "jk,ikd->ijd",
        sign_table(inner).astype(jnp.bfloat16),
        shaped,
        preferred_element_type=jnp.float32,
    )
    second = jnp.einsum(
        "hi,ijd->hjd", sign_table(outer).astype(jnp.float32), first, precision=lax.Precision.HIGHEST
    )
    return second.reshape(row_count, feat_width)


def precondition(factor_lower, residual):
    middle = lax.linalg.triangular_solve(
        factor_lower, residual[:, None], left_side=True, lower=True
    )
    return lax.linalg.triangular_solve(
        factor_lower, middle, left_side=True, lower=True, transpose_a=True
    )[:, 0]


def local(features, weights, labels, signs, samples, radius):
    highest = lax.Precision.HIGHEST
    row_count, feat_width = features.shape
    ex_count = lax.axis_size("ex")
    ex_index = lax.axis_index("ex")
    feat_index = lax.axis_index("feat")
    total_rows = row_count * ex_count
    sample_count = samples.shape[0]
    ridge = REG / D
    dense = features.astype(jnp.float32)
    margins = lax.psum(jnp.dot(dense, weights, precision=highest), "feat")
    probability = 1.0 / (1.0 + jnp.exp(-margins))
    curvature = probability * (1.0 - probability)
    grad_part = jnp.dot(probability - labels.astype(jnp.float32), dense, precision=highest)
    gradient = lax.psum(grad_part, "ex") / total_rows + ridge * weights
    weighted = (jnp.sqrt(curvature)[:, None] * dense).astype(jnp.bfloat16)
    weighted_float = weighted.astype(jnp.float32)
    signed = weighted * signs.astype(jnp.bfloat16)[:, None]
    mixed = local_mix(signed)
    for bit_index in range(ex_count.bit_length() - 1):
        partner = from_partner(mixed, "ex", bit_index)
        upper = ex_index >> bit_index & 1
        mixed = jnp.where(upper == 0, mixed + partner, partner - mixed)
    local_place = samples - ex_index * row_count
    owned = ((local_place >= 0) & (local_place < row_count)).astype(jnp.float32)
    picked = mixed[jnp.clip(local_place, 0, row_count - 1)] * owned[:, None]
    summed = lax.psum_scatter(picked, "ex", scatter_dimension=0, tiled=True)
    sketch = (summed * (1.0 / math.sqrt(total_rows * sample_count))).astype(jnp.bfloat16)
    wide_sketch = lax.all_gather(sketch, "feat", axis=1, tiled=True)
    piece = lax.all_gather(wide_sketch, "ex", axis=0, tiled=True)
    gram = lax.dot_general(
        piece, piece, (((0,), (0,)), ((), ())), preferred_element_type=jnp.float32
    )
    gram = gram + ridge * jnp.eye(D, dtype=jnp.float32)
    factor_lower = jnp.linalg.cholesky(gram)

    def apply_inverse(residual_part):
        gathered = lax.all_gather(residual_part, "feat", axis=0, tiled=True)
        return (gathered, precondition(factor_lower, gathered))

    solution = jnp.zeros((feat_width,), jnp.float32)
    residual = -gradient
    gathered, solved = apply_inverse(residual)
    inner_now = jnp.dot(gathered, solved)
    direction = solved
    for number in range(ITERS):
        dir_part = lax.dynamic_slice_in_dim(direction, feat_index * feat_width, feat_width, 0)
        row_part = jnp.dot(weighted_float, dir_part, precision=highest)
        row_sums = lax.psum(row_part, "feat")
        column_part = jnp.dot(row_sums, weighted_float, precision=highest)
        curved = lax.psum(column_part, "ex") / total_rows + ridge * dir_part
        curvature_sum = lax.psum(jnp.dot(dir_part, curved), "feat")
        step_size = inner_now / curvature_sum
        solution = solution + step_size * dir_part
        residual = residual - step_size * curved
        if number + 1 < ITERS:
            gathered, solved = apply_inverse(residual)
            inner_next = jnp.dot(gathered, solved)
            direction = solved + inner_next / inner_now * direction
            inner_now = inner_next
    length_sq = lax.psum(jnp.dot(solution, solution), "feat")
    scale_step = jnp.minimum(1.0, radius[0] * math.sqrt(D) / jnp.sqrt(length_sq + 1e-06))
    return weights + scale_step * solution


def solution(mesh):
    in_specs = (P("ex", "feat"), P("feat"), P("ex"), P("ex"), P(), P())
    out_specs = P("feat")
    return jax.shard_map(local, mesh=mesh, in_specs=in_specs, out_specs=out_specs, check_vma=False)
```

profile of v0, /device:TPU:1, one launch (start us, length us, event | category | flops | bytes accessed | tf_op | source)
XLA Modules:
  0.0 1996.8 jit_solution(15688813693721951574)
XLA Ops:
  52.7 90.9 %collective-permute-done.1 = f32[2048,512]{1,0:T(8,128)} collective-permute-done((f32[2048,512]{1,0:T(8,128)}, f32[2048,512]{1,0:T(8,128)}, u32[]{:S(2)}, u32[]{:S(2)}) %collective-permute-start.1) | collective-permute-done | bytes 4194336 | tf_op jit(solution)/shard_map/ppermute | solution.py:18
  152.8 89.9 %collective-permute-done.2 = f32[2048,512]{1,0:T(8,128)} collective-permute-done((f32[2048,512]{1,0:T(8,128)}, f32[2048,512]{1,0:T(8,128)}, u32[]{:S(2)}, u32[]{:S(2)}) %collective-permute-start.2) | collective-permute-done | bytes 4194336 | tf_op jit(solution)/shard_map/ppermute | solution.py:18
  250.5 89.0 %collective-permute-done.3 = f32[2048,512]{1,0:T(8,128)} collective-permute-done((f32[2048,512]{1,0:T(8,128)}, f32[2048,512]{1,0:T(8,128)}, u32[]{:S(2)}, u32[]{:S(2)}) %collective-permute-start.3) | collective-permute-done | bytes 4194336 | tf_op jit(solution)/shard_map/ppermute | solution.py:18
  348.8 87.9 %collective-permute-done.4 = f32[2048,512]{1,0:T(8,128)} collective-permute-done((f32[2048,512]{1,0:T(8,128)}, f32[2048,512]{1,0:T(8,128)}, u32[]{:S(2)}, u32[]{:S(2)}) %collective-permute-start.4) | collective-permute-done | bytes 4194336 | tf_op jit(solution)/shard_map/ppermute | solution.py:18
  443.1 11.7 gather_fusion
  459.5 82.9 %reduce-scatter.2.cloned.1.call-done = f32[64,512]{1,0:T(8,128)} async-done(((f32[2048,512]{1,0:T(8,128)}), f32[64,512]{1,0:T(8,128)}) %reduce-scatter.2.cloned.1.call-update) | async-done | bytes 131088 | tf_op jit(solution)/shard_map/reduce_scatter | solution.py:87
  556.4 68.1 %psum.106 = f32[512]{0:T(512)S(1)} all-reduce(f32[512]{0:T(512)S(1)} %bitcast.2138), channel_id=1, replica_groups=mesh['ex'=32,'feat'=4] {'ex'}, use_global_device_ids=true, to_apply=%region_1.0 | all-reduce | flops 512 | bytes 4096 | tf_op jit(solution)/shard_map/psum | solution.py:75
  633.0 24.3 %fusion.556 = f32[2048,2048]{1,0:T(8,128)} fusion(bf16[2048,2048]{1,0:T(8,128)(2,1)} %all-gather.6.cloned.1.call-done), kind=kOutput, calls=%fused_computation.1868 | convolution fusion | flops 17179869184 | bytes 25165824 | tf_op jit(solution)/shard_map/dot_general | solution.py:91
  657.3 17.6 copy.12
  674.9 12.3 fusion.1
  692.9 11.7 cholesky.456
  727.5 11.9 cholesky.479
  755.2 11.7 cholesky.502
  784.6 11.7 cholesky.523
  814.1 11.7 cholesky.960
  843.9 11.9 cholesky.980
  874.1 11.7 cholesky.1000
  904.8 11.7 cholesky.1020
  935.1 11.7 cholesky.1040
  965.3 11.7 cholesky.1060
  995.5 11.7 cholesky.1080
  1024.7 11.9 cholesky.1100
  1053.6 11.7 cholesky.1120
  1082.0 11.7 cholesky.1140
  1109.3 11.9 cholesky.1160
  1159.2 12.5 select_select_fusion
  1171.7 56.5 %while.16 = (s32[]{:T(128)}, f32[2048,2048]{1,0:T(8,128)}, s32[16,2]{0,1:T(2,128)S(1)}, f32[16,128,128]{2,1,0:T(8,128)}, s32[]{:T(128)}) while((s32[]{:T(128)}, f32[2048,2048]{1,0:T(8,128)}, s32[16,2]{0,1:T(2,128)S(1)}, f32[16,128,128]{2,1,0:T(8,128)}, s32[]{:T(128)}) %tuple.563), condition=%wide.while_cond.1, body=%wide.while_body.1.sunk | while | flops 2 | bytes 132705 | solution.py:56
  1228.2 158.4 %custom-call.151 = f32[16,128,128]{1,2,0:T(8,128)S(1)} custom-call(f32[16,128,128]{2,1,0:T(8,128)} %get-tuple-element.60), custom_call_target="InvertDiagBlocksLowerTriangular" | custom-call | tf_op jit(solution)/shard_map/triangular_solve/custom-call.32 | solution.py:56
  1449.6 67.6 %psum.108 = f32[512]{0:T(512)S(1)} all-reduce(f32[512]{0:T(512)S(1)} %bitcast.2139), channel_id=1, replica_groups=mesh['ex'=32,'feat'=4] {'ex'}, use_global_device_ids=true, to_apply=%region_36.39 | all-reduce | flops 512 | bytes 4096 | tf_op jit(solution)/shard_map/psum | solution.py:111
  1599.4 69.4 %psum.111 = f32[512]{0:T(512)S(1)} all-reduce(f32[512]{0:T(512)S(1)} %bitcast.2140), channel_id=1, replica_groups=mesh['ex'=32,'feat'=4] {'ex'}, use_global_device_ids=true, to_apply=%region_39.42 | all-reduce | flops 512 | bytes 4096 | tf_op jit(solution)/shard_map/psum | solution.py:111
  1750.2 69.4 %psum.114 = f32[512]{0:T(512)S(1)} all-reduce(f32[512]{0:T(512)S(1)} %bitcast.2141), channel_id=1, replica_groups=mesh['ex'=32,'feat'=4] {'ex'}, use_global_device_ids=true, to_apply=%region_42.45 | all-reduce | flops 512 | bytes 4096 | tf_op jit(solution)/shard_map/psum | solution.py:111
  1901.8 69.4 %psum.117 = f32[512]{0:T(512)S(1)} all-reduce(f32[512]{0:T(512)S(1)} %bitcast.2137), channel_id=1, replica_groups=mesh['ex'=32,'feat'=4] {'ex'}, use_global_device_ids=true, to_apply=%region_45.48 | all-reduce | flops 512 | bytes 4096 | tf_op jit(solution)/shard_map/psum | solution.py:111
  (925 shorter events, 763.1 us)
Async XLA Ops:
  6.5 535.8 %reduce-scatter.2.cloned.1.call-start = ((), (), s32[]{:S(2)}) async-start(), calls=%async_computation.1 | async-start | bytes 4325376 | tf_op jit(solution)/shard_map/reduce_scatter | solution.py:87
  35.1 9.8 collective-permute-start
  51.3 92.3 %collective-permute-start.1 = (f32[2048,512]{1,0:T(8,128)}, f32[2048,512]{1,0:T(8,128)}, u32[]{:S(2)}, u32[]{:S(2)}) collective-permute-start(f32[2048,512]{1,0:T(8,128)} %subtract_select_fusion.4), channel_id=1, source_target_pairs={{0,8},{4,12},{8,0},{12,4},{16,24},{20,28},{24,16},{28,20},{32,40},... | collective-permute-start | bytes 12582920 | tf_op jit(solution)/shard_map/ppermute | solution.py:18
  52.7 296.1 %copy-start.1 = (s32[2048]{0:T(1024)S(1)}, s32[2048]{0:T(1024)}, u32[]{:S(2)}) copy-start(s32[2048]{0:T(1024)} %param.14) | copy-start | bytes 24580
  150.1 92.7 %collective-permute-start.2 = (f32[2048,512]{1,0:T(8,128)}, f32[2048,512]{1,0:T(8,128)}, u32[]{:S(2)}, u32[]{:S(2)}) collective-permute-start(f32[2048,512]{1,0:T(8,128)} %subtract_select_fusion.3), channel_id=1, source_target_pairs={{0,16},{4,20},{8,24},{12,28},{16,0},{20,4},{24,8},{28,12},{32,48},... | collective-permute-start | bytes 12582920 | tf_op jit(solution)/shard_map/ppermute | solution.py:18
  249.2 90.3 %collective-permute-start.3 = (f32[2048,512]{1,0:T(8,128)}, f32[2048,512]{1,0:T(8,128)}, u32[]{:S(2)}, u32[]{:S(2)}) collective-permute-start(f32[2048,512]{1,0:T(8,128)} %subtract_select_fusion.2), channel_id=1, source_target_pairs={{0,32},{4,36},{8,40},{12,44},{16,48},{20,52},{24,56},{28,60},{32,0... | collective-permute-start | bytes 12582920 | tf_op jit(solution)/shard_map/ppermute | solution.py:18
  345.9 90.8 %collective-permute-start.4 = (f32[2048,512]{1,0:T(8,128)}, f32[2048,512]{1,0:T(8,128)}, u32[]{:S(2)}, u32[]{:S(2)}) collective-permute-start(f32[2048,512]{1,0:T(8,128)} %subtract_select_fusion.1), channel_id=1, source_target_pairs={{0,64},{4,68},{8,72},{12,76},{16,80},{20,84},{24,88},{28,92},{32,9... | collective-permute-start | bytes 12582920 | tf_op jit(solution)/shard_map/ppermute | solution.py:18
  443.1 181.3 %copy-start.2 = (f32[512]{0:T(512)S(1)}, f32[512]{0:T(512)}, u32[]{:S(2)}) copy-start(f32[512]{0:T(512)} %param.11) | copy-start | bytes 6148
  459.4 173.6 %all-gather.6.cloned.1.call-start = ((), (), s32[]{:S(2)}) async-start(), calls=%async_computation.2 | async-start | bytes 8650752 | tf_op jit(solution)/shard_map/all_gather | solution.py:90
  687.1 5.7 copy-start
Sparse Core Ops, SparseCore 0:
  459.5 82.7 reduce-scatter.1
  554.0 56.7 all-gather.5
where the time goes:
time: 2020 us; the launch traced here: 2000 us
  other arithmetic  586 us (29%)
  blocking collectives  460 us (23%)
  waiting for transfers between devices  448 us (22%)
  matrix products  346 us (17%)
  local copies, waits for them, and re-layouts  110 us (5%)
  between operations  36.2 us (2%)
    ppermute x5, waiting for transfers between devices, from_partner(): return lax.ppermute(value, axis, pairs)  365 us
    another operation x62, other arithmetic, local(): factor_lower = jnp.linalg.cholesky(gram)  356 us
    psum x4, blocking collectives, local(): curved = lax.psum(column_part, 'ex') / total_rows + ridge * dir_part  276 us
    another operation x4, other arithmetic, precondition(): lax.linalg.triangular_solve(factor_lower, middle, left_side=True, lower=T...  171 us
    another operation x124, matrix products, precondition(): lax.linalg.triangular_solve(factor_lower, residual[:, None], left_side=Tr...  107 us
    another operation x124, matrix products, precondition(): lax.linalg.triangular_solve(factor_lower, middle, left_side=True, lower=T...  99.2 us
    another operation x30, matrix products, local(): factor_lower = jnp.linalg.cholesky(gram)  92.6 us
    reduce_scatter x1, waiting for transfers between devices, local(): summed = lax.psum_scatter(picked, 'ex', scatter_dimension=0, tiled=True)  82.9 us
  transfers between devices with their start and end apart: 7, of which 6 were waited for; matrix products, arithmetic and copies ran while one was open for 0% of the time, Pallas kernels for 0%

commit v1 on v0

v1 whole, which is shorter than its diff:
```python
import math

import jax
import jax.numpy as jnp
from jax import lax
from jax.experimental import pallas as pl
from jax.experimental.pallas import tpu as pltpu
from jax.sharding import PartitionSpec as P

D = 2048
ITERS = 4
REG = 0.02
HI = lax.Precision.HIGHEST
NN = (((1,), (0,)), ((), ()))
NT = (((1,), (1,)), ((), ()))
TN = (((0,), (0,)), ((), ()))
MESH = pl.DeviceIdType.MESH

def split2(value):
    high = value.astype(jnp.bfloat16)
    return high, (value - high.astype(jnp.float32)).astype(jnp.bfloat16)


def block_inverse(block):
    lanes = lax.broadcasted_iota(jnp.int32, (1, 128), 1)
    subs = lax.broadcasted_iota(jnp.int32, (8, 128), 0)
    tiles = [block[8 * t : 8 * t + 8, :] for t in range(16)]
    column = [jnp.broadcast_to(tile[:, 0:1], (8, 128)) for tile in tiles]
    for k in range(128):
        t0, r = k // 8, k % 8
        pivot = jnp.broadcast_to(column[t0][r : r + 1, :], (8, 128))
        inverse = 1.0 / pivot
        scaled = [None] * 16
        for t in range(t0, 16):
            scaled[t] = column[t] * inverse
        scaled[t0] = jnp.where(subs > r, scaled[t0], 0.0)
        row = tiles[t0][r : r + 1, :]
        row = jnp.broadcast_to(jnp.where(lanes == k, row + row, row), (8, 128))
        if k + 1 < 128:
            ahead = [None] * 16
            for t in range(t0, 16):
                ahead[t] = jnp.broadcast_to(tiles[t][:, k + 1 : k + 2], (8, 128))
            cross = jnp.broadcast_to(ahead[t0][r : r + 1, :], (8, 128))
            column = [None] * 16
            for t in range(t0, 16):
                column[t] = ahead[t] - scaled[t] * cross
        for t in range(t0, 16):
            tiles[t] = tiles[t] - scaled[t] * row
    whole = jnp.concatenate(tiles, axis=0)
    rows = lax.broadcasted_iota(jnp.int32, (128, 128), 0)
    cols = lax.broadcasted_iota(jnp.int32, (128, 128), 1)
    diagonal = jnp.where(rows == cols, whole, 0.0)
    along_rows = jnp.sum(diagonal, axis=0, keepdims=True)
    along_cols = jnp.sum(diagonal, axis=1, keepdims=True)
    lower = jnp.where(cols <= rows, whole, 0.0)
    return lower * (1.0 / along_rows) * (1.0 / jnp.sqrt(along_cols))


def factor_kernel(sketch, up_hi, up_lo, inv_hi, inv_lo, gram, invs, trio_l, trio_r):
    ridge = REG / D
    for a in range(4):
        for b in range(a, 4):
            for h in range(2):
                part = lax.dot_general(
                    sketch[:, 512 * a + 256 * h : 512 * a + 256 * h + 256], sketch[:, 512 * b : 512 * b + 512], TN, preferred_element_type=jnp.float32
                )
                if a == b:
                    rows = lax.broadcasted_iota(jnp.int32, (256, 512), 0) + 256 * h
                    cols = lax.broadcasted_iota(jnp.int32, (256, 512), 1)
                    part = part + jnp.where(rows == cols, ridge, 0.0)
                gram[512 * a + 256 * h : 512 * a + 256 * h + 256, 512 * b : 512 * b + 512] = part

    def step(k, carry):
        at = pl.multiple_of(k * 128, 128)
        rows = pl.ds(at, 128)
        inverse = block_inverse(gram[rows, rows])
        invs[k] = inverse
        first = k // 4
        ih, il = split2(inverse)
        ileft = jnp.concatenate([ih, ih, il], axis=1)
        for c in range(4):

            @pl.when(c >= first)
            def _():
                cs = slice(512 * c, 512 * c + 512)
                gh, gl = split2(gram[rows, cs])
                panel = lax.dot_general(ileft, jnp.concatenate([gh, gl, gh], axis=0), NN, preferred_element_type=jnp.float32)
                cols = lax.broadcasted_iota(jnp.int32, (128, 512), 1) + 512 * c
                panel = jnp.where(cols >= at + 128, panel, 0.0)
                gram[rows, cs] = panel
                ph, plo = split2(panel)
                trio_r[0:128, cs] = ph
                trio_r[128:256, cs] = plo
                trio_r[256:384, cs] = ph
                trio_l[0:128, cs] = ph
                trio_l[128:256, cs] = ph
                trio_l[256:384, cs] = plo

        for a in range(4):

            @pl.when(a >= first)
            def _():
                ra = slice(512 * a, 512 * a + 512)
                for b in range(a, 4):
                    cs = slice(512 * b, 512 * b + 512)
                    gram[ra, cs] = gram[ra, cs] - lax.dot_general(trio_l[:, ra], trio_r[:, cs], TN, preferred_element_type=jnp.float32)

        return carry

    lax.fori_loop(0, 16, step, 0)

    def chunk(a, carry):
        at = pl.multiple_of(a * 512, 512)

        def up(i, j, size):
            return gram[pl.ds(pl.multiple_of(at + i, 128), size), pl.ds(pl.multiple_of(at + j, 128), size)]

        def join(top, bottom, cross):
            middle = lax.dot_general(cross, top, TN, precision=HI, preferred_element_type=jnp.float32)
            corner = -lax.dot_general(bottom, middle, NN, precision=HI, preferred_element_type=jnp.float32)
            zero = jnp.zeros_like(top)
            return jnp.concatenate([jnp.concatenate([top, zero], axis=1), jnp.concatenate([corner, bottom], axis=1)], axis=0)

        q = [invs[4 * a + i] for i in range(4)]
        one = join(q[0], q[1], up(0, 128, 128))
        two = join(q[2], q[3], up(256, 384, 128))
        whole = join(one, two, up(0, 256, 256))
        hi, lo = split2(whole)
        inv_hi[a] = hi
        inv_lo[a] = lo
        hi, lo = split2(gram[pl.ds(at, 512), :])
        up_hi[pl.ds(at, 512), :] = hi
        up_lo[pl.ds(at, 512), :] = lo
        return carry

    lax.fori_loop(0, 4, chunk, 0)


def factor(sketch):
    vm = pl.BlockSpec(memory_space=pltpu.VMEM)
    return pl.pallas_call(
        factor_kernel,
        out_shape=(
            jax.ShapeDtypeStruct((D, D), jnp.bfloat16),
            jax.ShapeDtypeStruct((D, D), jnp.bfloat16),
            jax.ShapeDtypeStruct((4, 512, 512), jnp.bfloat16),
            jax.ShapeDtypeStruct((4, 512, 512), jnp.bfloat16),
        ),
        in_specs=[vm],
        out_specs=(vm, vm, vm, vm),
        scratch_shapes=[
            pltpu.VMEM((D, D), jnp.float32),
            pltpu.VMEM((16, 128, 128), jnp.float32),
            pltpu.VMEM((384, D), jnp.bfloat16),
            pltpu.VMEM((384, D), jnp.bfloat16),
        ],
        compiler_params=pltpu.CompilerParams(vmem_limit_bytes=60 * 2**20),
        name="factor",
    )(sketch)


def pieces(row):
    first = row.astype(jnp.bfloat16).astype(jnp.float32)
    rest = row - first
    second = rest.astype(jnp.bfloat16).astype(jnp.float32)
    third = rest - second
    which = lax.broadcasted_iota(jnp.int32, (16, row.shape[1]), 0)
    stacked = jnp.where(which == 0, first, jnp.where(which == 1, second, jnp.where(which == 2, third, 0.0)))
    return stacked.astype(jnp.bfloat16)


def row_times(row, matrix, dims):
    return jnp.sum(lax.dot_general(pieces(row), matrix, dims, preferred_element_type=jnp.float32), axis=0, keepdims=True)


def pcg_kernel(total_rows, weighted, grad, up_hi, up_lo, inv_hi, inv_lo, weights, radius, out, full, zbuf, abuf, bbuf, zs, zr, a_s, a_r, b_s, b_r):
    ex = lax.axis_index("ex")
    feat = lax.axis_index("feat")
    plane, within = ex // 8, ex % 8
    ridge = REG / D
    own = pl.ds(pl.multiple_of(feat * 512, 512), 512)

    def near(o):
        return (plane * 8 + (within + o) % 8, feat)

    def far(o):
        other = (plane * 4 + feat + o) % 16
        return ((other // 4) * 8 + within, other % 4)

    def along(o):
        return (ex, (feat + o) % 4)

    barrier = pltpu.get_barrier_semaphore()
    for o in range(1, 8):
        pl.semaphore_signal(barrier, inc=1, device_id=near(o), device_id_type=MESH)
    for o in range(1, 16):
        pl.semaphore_signal(barrier, inc=1, device_id=far(o), device_id_type=MESH)
    pl.semaphore_wait(barrier, 22)

    def exchange(value, buf, turn, me, count, peer, send, recv):
        buf[turn, me] = value
        copies = [
            pltpu.make_async_remote_copy(
                src_ref=buf.at[turn, me],
                dst_ref=buf.at[turn, me],
                send_sem=send.at[turn, o],
                recv_sem=recv.at[turn, o],
                device_id=peer(o),
                device_id_type=MESH,
            )
            for o in range(1, count)
        ]
        for copy in copies:
            copy.start()
        for copy in copies:
            copy.wait()

    def over_examples(part, turn):
        exchange(part, abuf, turn, within, 8, near, a_s, a_r)
        total = abuf[turn, 0]
        for q in range(1, 8):
            total = total + abuf[turn, q]
        exchange(total, bbuf, turn, plane * 4 + feat, 16, far, b_s, b_r)
        parts = []
        for z in range(4):
            parts.append((bbuf[turn, z] + bbuf[turn, 4 + z]) + (bbuf[turn, 8 + z] + bbuf[turn, 12 + z]))
        return jnp.concatenate(parts, axis=1)

    def over_features(part, turn):
        exchange(part, zbuf, turn, feat, 4, along, zs, zr)
        return (zbuf[turn, 0] + zbuf[turn, 1]) + (zbuf[turn, 2] + zbuf[turn, 3])

    def times(row, high, low, dims):
        high_row = row.astype(jnp.bfloat16).astype(jnp.float32)
        which = lax.broadcasted_iota(jnp.int32, (16, row.shape[1]), 0)
        stacked = jnp.where(which == 0, high_row, jnp.where(which == 1, row - high_row, 0.0)).astype(jnp.bfloat16)
        product = lax.dot_general(stacked, high, dims, preferred_element_type=jnp.float32)
        product = product + lax.dot_general(stacked, low, dims, preferred_element_type=jnp.float32)
        return jnp.sum(product, axis=0, keepdims=True)

    def solve(row):
        rest = row
        middle = []
        for a in range(4):
            part = times(rest[:, :512], inv_hi[a], inv_lo[a], NT)
            middle.append(part)
            if a < 3:
                here, right = slice(512 * a, 512 * a + 512), slice(512 * a + 512, D)
                rest = rest[:, 512:] - times(part, up_hi[here, right], up_lo[here, right], NN)
        rest = jnp.concatenate(middle, axis=1)
        result = []
        for a in range(3, -1, -1):
            part = times(rest[:, 512 * a :], inv_hi[a], inv_lo[a], NN)
            result.insert(0, part)
            if a > 0:
                above, here = slice(0, 512 * a), slice(512 * a, 512 * a + 512)
                rest = rest[:, : 512 * a] - times(part, up_hi[above, here], up_lo[above, here], NT)
        return jnp.concatenate(result, axis=1)

    def dot(left, right):
        return jnp.sum(left * right, axis=1, keepdims=True)

    residual = -over_examples(grad[...] * (1.0 / total_rows) + weights[...] * (ridge / 32), 0)

    def step(number, carry):
        answer, residual, direction, inner = carry
        solved = solve(residual)
        inner_now = dot(residual, solved)
        direction = solved + jnp.where(number == 0, 0.0, inner_now / inner) * direction
        full[...] = direction
        row_sums = over_features(row_times(full[:, own], weighted[...], NT), number)
        product = over_examples(row_times(row_sums, weighted[...], NN), number + 1)
        curved = product * (1.0 / total_rows) + ridge * direction
        step_size = inner_now / dot(direction, curved)
        return answer + step_size * direction, residual - step_size * curved, direction, inner_now

    zero = jnp.zeros((1, D), jnp.float32)
    answer = lax.fori_loop(0, ITERS, step, (zero, residual, zero, jnp.ones((1, 1), jnp.float32)))[0]
    scale = jnp.minimum(1.0, radius[...] * math.sqrt(D) / jnp.sqrt(dot(answer, answer) + 1e-06))
    full[...] = answer
    out[...] = weights[...] + scale * full[:, own]


def pcg(total_rows, weighted, grad, factors, weights, radius):
    vm = pl.BlockSpec(memory_space=pltpu.VMEM)
    dma = pltpu.SemaphoreType.DMA
    return pl.pallas_call(
        lambda *refs: pcg_kernel(total_rows, *refs),
        out_shape=jax.ShapeDtypeStruct((1, 512), jnp.float32),
        in_specs=[vm] * 8,
        out_specs=vm,
        scratch_shapes=[
            pltpu.VMEM((1, D), jnp.float32),
            pltpu.VMEM((4, 4, 1, D), jnp.float32),
            pltpu.VMEM((5, 8, 1, 512), jnp.float32),
            pltpu.VMEM((5, 16, 1, 512), jnp.float32),
            dma((4, 4)),
            dma((4, 4)),
            dma((5, 8)),
            dma((5, 8)),
            dma((5, 16)),
            dma((5, 16)),
        ],
        compiler_params=pltpu.CompilerParams(vmem_limit_bytes=48 * 2**20, collective_id=0, has_side_effects=True),
        name="pcg",
    )(weighted, grad, *factors, weights, radius)


def parity(common):
    for shift in (8, 4, 2, 1):
        common = common ^ (common >> shift)
    return 1 - 2 * (common & 1)


def local(features, weights, labels, signs, samples, radius):
    row_count, feat_width = features.shape
    ex_count = lax.axis_size("ex")
    ex_index = lax.axis_index("ex")
    total_rows = row_count * ex_count
    sample_count = samples.shape[0]
    dense = features.astype(jnp.float32)
    margins = lax.psum(jnp.dot(dense, weights, precision=HI), "feat")
    probability = 1.0 / (1.0 + jnp.exp(-margins))
    curvature = probability * (1.0 - probability)
    grad_part = jnp.dot(probability - labels.astype(jnp.float32), dense, precision=HI)
    weighted = (jnp.sqrt(curvature)[:, None] * dense).astype(jnp.bfloat16)
    signed = weighted * signs.astype(jnp.bfloat16)[:, None]
    low, high = samples % row_count, samples // row_count
    coarse = parity((low[:, None] // 128) & lax.iota(jnp.int32, row_count // 128)[None, :])
    coarse = coarse * parity(high & ex_index)[:, None]
    fine = parity((low[:, None] % 128) & lax.iota(jnp.int32, 128)[None, :])
    pattern = (coarse.astype(jnp.bfloat16)[:, :, None] * fine.astype(jnp.bfloat16)[:, None, :]).reshape(sample_count, row_count)
    picked = lax.dot_general(pattern, signed, NN, preferred_element_type=jnp.float32)
    summed = lax.psum_scatter(picked, "ex", scatter_dimension=0, tiled=True)
    sketch = (summed * (1.0 / math.sqrt(total_rows * sample_count))).astype(jnp.bfloat16)
    wide = lax.all_gather(sketch, "feat", axis=1, tiled=True)
    whole = lax.all_gather(wide, "ex", axis=0, tiled=True)
    factors = factor(whole)
    out = pcg(total_rows, weighted, grad_part[None, :], factors, weights[None, :], radius[None, :])
    return out[0]


def solution(mesh):
    in_specs = (P("ex", "feat"), P("feat"), P("ex"), P("ex"), P(), P())
    return jax.shard_map(local, mesh=mesh, in_specs=in_specs, out_specs=P("feat"), check_vma=False)
```

time: 2020 us -> 507 us (0.25); the launches traced: 2000 us -> 507 us
  other arithmetic: 586 us -> 14.5 us
  blocking collectives: 460 us -> 21.5 us
  matrix products: 346 us -> 12.1 us
  waiting for transfers between devices: 448 us -> 135 us
  Pallas kernels: 0 us -> 307 us
  local copies, waits for them, and re-layouts: 110 us -> 2.46 us
  between operations: 36.2 us -> 14.2 us
    another operation x66 -> x0, other arithmetic: 527 us -> none  [the longest x62 356 us: local(): factor_lower = jnp.linalg.cholesky(gram)]
    psum x15 -> x1, blocking collectives: 417 us -> 10.7 us  [local(): margins = lax.psum(jnp.dot(dense, weights, precision=HI), 'feat')]
    ppermute x5 -> x0, waiting for transfers between devices: 365 us -> none  [from_partner(): return lax.ppermute(value, axis, pairs)]
    pallas_call x0 -> x2, Pallas kernels: none -> 307 us  [the longest x1 214 us: factor(): pl.pallas_call(factor_kernel, out_shape=(jax.ShapeDtypeStruct((D, D), jnp...]
    another operation x278 -> x0, matrix products: 298 us -> none  [the longest x124 107 us: precondition(): lax.linalg.triangular_solve(factor_lower, residual[:, None], left_side=Tr...]
    another operation x113 -> x0, local copies, waits for them, and re-layouts: 64.8 us -> none  [the longest x97 56.9 us: precondition(): lax.linalg.triangular_solve(factor_lower, middle, left_side=True, lower=T...]
    all_gather x1, waiting for transfers between devices: 0.01 us -> 53.4 us  [local(): whole = lax.all_gather(wide, 'ex', axis=0, tiled=True)]
    dot_general x13 -> x3, matrix products: 47.2 us -> 12.1 us  [the longest x1 6.32 us: local(): lax.dot_general(pattern, signed, NN, preferred_element_type=jnp.float32)]
  transfers between devices with their start and end apart: 7 -> 2, of which waited for: 6 -> 2; matrix products, arithmetic and copies ran while one was open for 0% -> 0% of each run, Pallas kernels for 0% -> 0%
where the time goes in v1:
time: 507 us
  Pallas kernels  307 us (61%)
  waiting for transfers between devices  135 us (27%)
  blocking collectives  21.5 us (4%)
  other arithmetic  14.5 us (3%)
  between operations  14.2 us (3%)
  matrix products  12.1 us (2%)
    pallas_call x1, Pallas kernels, factor(): pl.pallas_call(factor_kernel, out_shape=(jax.ShapeDtypeStruct((D, D), jnp...  214 us
    pallas_call x1, Pallas kernels, pcg(): pl.pallas_call(lambda *refs: pcg_kernel(total_rows, *refs), out_shape=jax...  92.9 us
    reduce_scatter x1, waiting for transfers between devices, local(): summed = lax.psum_scatter(picked, 'ex', scatter_dimension=0, tiled=True)  81.5 us
    all_gather x1, waiting for transfers between devices, local(): whole = lax.all_gather(wide, 'ex', axis=0, tiled=True)  53.4 us
    all_gather x1, blocking collectives, local(): wide = lax.all_gather(sketch, 'feat', axis=1, tiled=True)  10.8 us
    mul x1, other arithmetic, local(): coarse.astype(jnp.bfloat16)[:, :, None]  10.8 us
    psum x1, blocking collectives, local(): margins = lax.psum(jnp.dot(dense, weights, precision=HI), 'feat')  10.7 us
  transfers between devices with their start and end apart: 2, of which 2 were waited for; matrix products, arithmetic and copies ran while one was open for 0% of the time, Pallas kernels for 0%

profile of v1, /device:TPU:1, one launch (start us, length us, event | category | flops | bytes accessed | tf_op | source)
XLA Modules:
  0.0 506.9 jit_solution(6153123097014054328)
XLA Ops:
  6.5 0.0 copy-start.3
  6.5 0.0 reduce-scatter.2.cloned.1.call-start
  6.5 3.3 fusion.23
  9.9 10.7 %psum.7 = f32[2048]{0:T(1024)S(1)} all-reduce(f32[2048]{0:T(1024)S(1)} %bitcast.20), channel_id=1, replica_groups=mesh['ex'=32,'feat'=4] {'feat'}, use_global_device_ids=true, to_apply=%region_0.0 | all-reduce | flops 2048 | bytes 16384 | tf_op jit(solution)/shard_map/psum | solution.py:322
  20.5 0.0 copy-done.3
  20.6 0.0 copy-start.4
  20.6 0.0 copy-start.2
  20.6 2.1 multiply_convert_fusion.refs_0_
  22.7 0.0 copy-done.4
  22.7 0.7 fusion.7
  23.4 0.1 fusion.13
  23.5 0.3 copy.7
  23.7 0.0 copy-done.2
  23.8 10.8 %broadcast_multiply_fusion = bf16[2048,16,128]{2,1,0:T(8,128)(2,1)S(1)} fusion(bf16[2048,128]{1,0:T(8,128)(2,1)S(1)} %fusion.7, bf16[2048,16]{1,0:T(8,128)(2,1)S(1)} %copy.7), kind=kLoop, calls=%fused_computation.3 | loop fusion | flops 4194304 | bytes 8978432 | tf_op jit(solution)/shard_map/mul | solution.py:332
  34.5 6.3 %fusion = f32[2048,512]{1,0:T(8,128)} fusion(bf16[256,8,16,128]{3,2,1,0:T(8,128)(2,1)S(1)} %bitcast.19, bf16[2048,512]{1,0:T(8,128)(2,1)S(1)} %multiply_convert_fusion.refs_0_, bf16[2048]{0:T(1024)(128)(2,1)S(1)} %convert_element_type.34), kind=kOutput, calls=%fused_computation | convolution fusion | flops 4296015872 | bytes 14684160 | tf_op jit(solution)/shard_map/dot_general | solution.py:333
  40.9 0.0 reduce-scatter.2.cloned.1.call-update
  40.9 0.0 all-gather.2.cloned.1.call-start
  40.9 81.5 %reduce-scatter.2.cloned.1.call-done = f32[64,512]{1,0:T(8,128)} async-done(((f32[2048,512]{1,0:T(8,128)}), f32[64,512]{1,0:T(8,128)}) %reduce-scatter.2.cloned.1.call-update) | async-done | bytes 131088 | tf_op jit(solution)/shard_map/reduce_scatter | solution.py:334
  122.4 0.9 multiply_convert_fusion.1
  123.4 10.8 %all_gather.6 = bf16[64,2048]{1,0:T(8,128)(2,1)} all-gather(bf16[64,512]{1,0:T(8,128)(2,1)S(1)} %multiply_convert_fusion.1), channel_id=1, replica_groups=mesh['ex'=32,'feat'=4] {'feat'}, dimensions={1}, use_global_device_ids=true | all-gather | bytes 327680 | tf_op jit(solution)/shard_map/all_gather | solution.py:336
  134.2 0.0 all-gather.2.cloned.1.call-update
  134.8 2.5 fusion.24.refs_1_
  137.3 0.0 copy-start.1
  137.3 53.4 %all-gather.2.cloned.1.call-done.sketch = bf16[2048,2048]{1,0:T(8,128)(2,1)} async-done(((bf16[64,2048]{1,0:T(8,128)(2,1)}), bf16[2048,2048]{1,0:T(8,128)(2,1)}) %all-gather.2.cloned.1.call-update) | async-done | bytes 8388624 | tf_op jit(solution)/shard_map/all_gather | solution.py:337
  190.7 214.2 %factor.1 = (bf16[2048,2048]{1,0:T(8,128)(2,1)}, bf16[2048,2048]{1,0:T(8,128)(2,1)}, bf16[4,512,512]{2,1,0:T(8,128)(2,1)}, bf16[4,512,512]{2,1,0:T(8,128)(2,1)}) custom-call(bf16[2048,2048]{1,0:T(8,128)(2,1)} %all-gather.2.cloned.1.call-done.sketch), custom_call_target="tpu_custom_call" | custom-call | tf_op jit(solution)/shard_map/factor/pallas_call | solution.py:141
  405.0 0.0 copy-done.1
  405.0 0.0 copy-start
  405.0 1.6 copy-done
  406.6 92.9 %pcg.1 = f32[1,512]{1,0:T(1,128)S(1)} custom-call(bf16[2048,512]{1,0:T(8,128)(2,1)S(1)} %multiply_convert_fusion.refs_0_, f32[1,512]{1,0:T(1,128)S(1)} %fusion.24.refs_1_, bf16[2048,2048]{1,0:T(8,128)(2,1)} %get-tuple-element.9.refs_2_, bf16[2048,2048]{1,0:T(8,128)(2,1)} %get-tuple-element.10.refs_3_, bf16[4,512,512]{2,1,0:T(8,128)(2,1)S(1)} %copy-done, ...), custom_call_target="tpu_custom_call" | custom-call | tf_op jit(solution)/shard_map/pcg/pallas_call | solution.py:287
  499.5 0.6 copy.15
  (3 shorter events, 0.0 us)
Async XLA Ops:
  6.5 14.0 %copy-start.3 = (s32[2048]{0:T(1024)S(1)}, s32[2048]{0:T(1024)}, u32[]{:S(2)}) copy-start(s32[2048]{0:T(1024)} %param.8) | copy-start | bytes 24580
  6.5 115.9 %reduce-scatter.2.cloned.1.call-start = ((), (), s32[]{:S(2)}) async-start(), calls=%async_computation.1 | async-start | bytes 4325376 | tf_op jit(solution)/shard_map/reduce_scatter | solution.py:334
  20.6 2.1 copy-start.4
  20.6 3.2 copy-start.2
  40.9 149.9 %all-gather.2.cloned.1.call-start = ((), (), s32[]{:S(2)}) async-start(), calls=%async_computation.2 | async-start | bytes 8650752 | tf_op jit(solution)/shard_map/all_gather | solution.py:337
  137.3 267.7 %copy-start.1 = (f32[512]{0:T(512)S(1)}, f32[512]{0:T(512)}, u32[]{:S(2)}) copy-start(f32[512]{0:T(512)} %param.7) | copy-start | bytes 6148
  405.0 1.6 copy-start
Sparse Core Ops, SparseCore 0:
  41.0 81.4 reduce-scatter.1
  134.3 56.3 all-gather.1

commit v2 on v1

--- a/solution.py
+++ b/solution.py
@@ -25,27 +25,73 @@
     lanes = lax.broadcasted_iota(jnp.int32, (1, 128), 1)
     subs = lax.broadcasted_iota(jnp.int32, (8, 128), 0)
     tiles = [block[8 * t : 8 * t + 8, :] for t in range(16)]
-    column = [jnp.broadcast_to(tile[:, 0:1], (8, 128)) for tile in tiles]
-    for k in range(128):
-        t0, r = k // 8, k % 8
-        pivot = jnp.broadcast_to(column[t0][r : r + 1, :], (8, 128))
-        inverse = 1.0 / pivot
-        scaled = [None] * 16
-        for t in range(t0, 16):
-            scaled[t] = column[t] * inverse
-        scaled[t0] = jnp.where(subs > r, scaled[t0], 0.0)
-        row = tiles[t0][r : r + 1, :]
-        row = jnp.broadcast_to(jnp.where(lanes == k, row + row, row), (8, 128))
-        if k + 1 < 128:
-            ahead = [None] * 16
-            for t in range(t0, 16):
-                ahead[t] = jnp.broadcast_to(tiles[t][:, k + 1 : k + 2], (8, 128))
-            cross = jnp.broadcast_to(ahead[t0][r : r + 1, :], (8, 128))
-            column = [None] * 16
-            for t in range(t0, 16):
-                column[t] = ahead[t] - scaled[t] * cross
-        for t in range(t0, 16):
-            tiles[t] = tiles[t] - scaled[t] * row
+
+    def lane(t, at):
+        return jnp.broadcast_to(tiles[t][:, at : at + 1], (8, 128))
+
+    def sub(tile, at):
+        return jnp.broadcast_to(tile[at : at + 1, :], (8, 128))
+
+    own = [lane(0, j) for j in range(8)]
+    nxt = [lane(1, j) for j in range(8)]
+    for g in range(16):
+        base = 8 * g
+        more, most = g + 1 < 16, g + 2 < 16
+        if more:
+            own_later = [lane(g + 1, base + 8 + j) for j in range(8)]
+        if most:
+            nxt_later = [lane(g + 2, base + 8 + j) for j in range(8)]
+            second = [lane(g + 2, base + j) for j in range(8)]
+        inverses, crosses, rows = [], {}, []
+        head = tiles[g]
+        nxt_scaled, second_scaled = [], []
+        for j in range(8):
+            inverse = 1.0 / sub(own[j], j)
+            inverses.append(inverse)
+            scaled = jnp.where(subs > j, own[j] * inverse, 0.0)
+            if more:
+                nxt_scaled.append(nxt[j] * inverse)
+            if most:
+                second_scaled.append(second[j] * inverse)
+            for i in range(j + 1, 8):
+                cross = sub(own[i], j)
+                crosses[j, i] = cross
+                own[i] = own[i] - scaled * cross
+                if more:
+                    nxt[i] = nxt[i] - nxt_scaled[j] * cross
+                if most:
+                    second[i] = second[i] - second_scaled[j] * cross
+            if more:
+                for i in range(8):
+                    cross = sub(nxt[j], i)
+                    own_later[i] = own_later[i] - nxt_scaled[j] * cross
+                    if most:
+                        nxt_later[i] = nxt_later[i] - second_scaled[j] * cross
+            row = head[j : j + 1, :]
+            row = jnp.broadcast_to(jnp.where(lanes == base + j, row + row, row), (8, 128))
+            rows.append(row)
+            head = head - scaled * row
+        tiles[g] = head
+        for t in range(g + 1, 16):
+            if t == g + 1:
+                scaled = nxt_scaled
+            elif t == g + 2:
+                scaled = second_scaled
+            else:
+                column = [lane(t, base + j) for j in range(8)]
+                scaled = []
+                for j in range(8):
+                    scaled.append(column[j] * inverses[j])
+                    for i in range(j + 1, 8):
+                        column[i] = column[i] - scaled[j] * crosses[j, i]
+            tile = tiles[t]
+            for j in range(8):
+                tile = tile - scaled[j] * rows[j]
+            tiles[t] = tile
+        if more:
+            own = own_later
+        if most:
+            nxt = nxt_later
     whole = jnp.concatenate(tiles, axis=0)
     rows = lax.broadcasted_iota(jnp.int32, (128, 128), 0)
     cols = lax.broadcasted_iota(jnp.int32, (128, 128), 1)
@@ -56,19 +102,26 @@
     return lower * (1.0 / along_rows) * (1.0 / jnp.sqrt(along_cols))
 
 
-def factor_kernel(sketch, up_hi, up_lo, inv_hi, inv_lo, gram, invs, trio_l, trio_r):
+def factor_kernel(left, right, up_hi, up_lo, inv_hi, inv_lo, gram, invs, trio_l, trio_r):
     ridge = REG / D
+    halves = (left, right)
     for a in range(4):
         for b in range(a, 4):
             for h in range(2):
-                part = lax.dot_general(
-                    sketch[:, 512 * a + 256 * h : 512 * a + 256 * h + 256], sketch[:, 512 * b : 512 * b + 512], TN, preferred_element_type=jnp.float32
-                )
-                if a == b:
-                    rows = lax.broadcasted_iota(jnp.int32, (256, 512), 0) + 256 * h
-                    cols = lax.broadcasted_iota(jnp.int32, (256, 512), 1)
-                    part = part + jnp.where(rows == cols, ridge, 0.0)
-                gram[512 * a + 256 * h : 512 * a + 256 * h + 256, 512 * b : 512 * b + 512] = part
+                for side in range(h if a == b else 0, 2):
+                    part = lax.dot_general(
+                        halves[h][:, 256 * a : 256 * a + 256],
+                        halves[side][:, 256 * b : 256 * b + 256],
+                        TN,
+                        preferred_element_type=jnp.float32,
+                    )
+                    if a == b and h == side:
+                        rows = lax.broadcasted_iota(jnp.int32, (256, 256), 0)
+                        cols = lax.broadcasted_iota(jnp.int32, (256, 256), 1)
+                        part = part + jnp.where(rows == cols, ridge, 0.0)
+                    gram[512 * a + 256 * h : 512 * a + 256 * h + 256, 512 * b + 256 * side : 512 * b + 256 * side + 256] = part
+                    if a == b and h < side:
+                        gram[512 * a + 256 : 512 * a + 512, 512 * a : 512 * a + 256] = jnp.zeros((256, 256), jnp.float32)
 
     def step(k, carry):
         at = pl.multiple_of(k * 128, 128)
@@ -136,7 +189,7 @@
     lax.fori_loop(0, 4, chunk, 0)
 
 
-def factor(sketch):
+def factor(left, right):
     vm = pl.BlockSpec(memory_space=pltpu.VMEM)
     return pl.pallas_call(
         factor_kernel,
@@ -146,7 +199,7 @@
             jax.ShapeDtypeStruct((4, 512, 512), jnp.bfloat16),
             jax.ShapeDtypeStruct((4, 512, 512), jnp.bfloat16),
         ),
-        in_specs=[vm],
+        in_specs=[vm, vm],
         out_specs=(vm, vm, vm, vm),
         scratch_shapes=[
             pltpu.VMEM((D, D), jnp.float32),
@@ -156,7 +209,7 @@
         ],
         compiler_params=pltpu.CompilerParams(vmem_limit_bytes=60 * 2**20),
         name="factor",
-    )(sketch)
+    )(left, right)
 
 
 def pieces(row):
@@ -306,6 +359,181 @@
     )(weighted, grad, *factors, weights, radius)
 
 
+def sketch_kernel(scale, signed, coarse, fine, left, right, send, keep, arrive, narrow, xin, yin, stage, xlast, ylast, mine, ssem, rsem, lsem):
+    ex = lax.axis_index("ex")
+    z = lax.axis_index("feat")
+    y, x, c = ex // 8, (ex // 2) % 4, ex % 2
+
+    def to_x(o):
+        return ((y * 4 + (x + o) % 4) * 2 + c, z)
+
+    def to_y(o):
+        return ((((y + o) % 4) * 4 + x) * 2 + c, z)
+
+    def to_z(o):
+        return (ex, (z + o) % 4)
+
+    other = (ex + 1 - 2 * c, z)
+    barrier = pltpu.get_barrier_semaphore()
+    for o in range(1, 4):
+        for peer in (to_x, to_y, to_z):
+            pl.semaphore_signal(barrier, inc=1, device_id=peer(o), device_id_type=MESH)
+    pl.semaphore_signal(barrier, inc=1, device_id=other, device_id_type=MESH)
+
+    started = []
+
+    def ship(src, dst, device):
+        at = len(started)
+        copy = pltpu.make_async_remote_copy(
+            src_ref=src, dst_ref=dst, send_sem=ssem.at[at], recv_sem=rsem.at[at], device_id=device, device_id_type=MESH
+        )
+        copy.start()
+        started.append(copy)
+        return copy
+
+    def mixed(row):
+        rows = pl.ds(pl.multiple_of(row, 256), 256)
+        fine_rows = fine[rows, :]
+        pattern = jnp.concatenate([fine_rows * jnp.broadcast_to(coarse[rows, h : h + 1], (256, 128)) for h in range(16)], axis=1)
+        return jnp.dot(pattern, signed[...], preferred_element_type=jnp.float32)
+
+    halves = []
+    for q in range(4):
+        send[q] = mixed((1 - c) * 1024 + 256 * q)
+        if q == 0:
+            pl.semaphore_wait(barrier, 10)
+        halves.append(ship(send.at[q], arrive.at[q], other))
+    for q in range(4):
+        keep[q] = mixed(c * 1024 + 256 * q)
+    for q in range(4):
+        halves[q].wait_recv()
+        total = keep[q] + arrive[q]
+        keep[q] = total
+        narrow[0, q] = total[:, :256].astype(jnp.bfloat16)
+        narrow[1, q] = total[:, 256:].astype(jnp.bfloat16)
+    first = []
+    for o in range(1, 4):
+        first.append(ship(narrow.at[0, (x + o) % 4], xin.at[o - 1], to_x(o)))
+        first.append(ship(narrow.at[1, (y + o) % 4], yin.at[o - 1], to_y(o)))
+    for copy in first:
+        copy.wait_recv()
+    left_total = keep[x, :, :256]
+    right_total = keep[y, :, 256:]
+    for o in range(3):
+        left_total = left_total + xin[o].astype(jnp.float32)
+        right_total = right_total + yin[o].astype(jnp.float32)
+    for q in range(4):
+        stage[0, q] = left_total[64 * q : 64 * q + 64, :]
+        stage[1, q] = right_total[64 * q : 64 * q + 64, :]
+    second = []
+    for o in range(1, 4):
+        second.append(ship(stage.at[0, (y + o) % 4], ylast.at[o - 1], to_y(o)))
+        second.append(ship(stage.at[1, (x + o) % 4], xlast.at[o - 1], to_x(o)))
+    for copy in second:
+        copy.wait_recv()
+    mine[0] = ((stage[0, y] + ylast[0] + ylast[1] + ylast[2]) * scale).astype(jnp.bfloat16)
+    mine[1] = ((stage[1, x] + xlast[0] + xlast[1] + xlast[2]) * scale).astype(jnp.bfloat16)
+
+    cols = pl.ds(pl.multiple_of(z * 256, 256), 256)
+    big, small = pl.ds(0, 48), pl.ds(48, 16)
+    every = pl.ds(0, 4)
+    own_left = pltpu.make_async_copy(mine.at[0], left.at[c, x, y, :, cols], lsem.at[0])
+    own_right = pltpu.make_async_copy(mine.at[1], right.at[c, y, x, :, cols], lsem.at[1])
+    own_left.start()
+    own_right.start()
+
+    def pass_on(work):
+        copies = []
+        for o in range(1, 4):
+            for src, dst, peer in work:
+                copies.append(ship(src, dst, peer(o)))
+        return copies
+
+    def same(ref, peer):
+        return (ref, ref, peer)
+
+    here_left, here_right = left.at[c, x, y], right.at[c, y, x]
+    copies = pass_on(
+        [
+            (mine.at[0, big], left.at[c, x, y, big, cols], to_z),
+            (mine.at[1, big], right.at[c, y, x, big, cols], to_z),
+            (mine.at[0, small], left.at[c, x, y, small, cols], to_y),
+            (mine.at[1, small], right.at[c, y, x, small, cols], to_x),
+        ]
+    )
+    own_left.wait()
+    own_right.wait()
+    for copy in copies:
+        copy.wait_recv()
+    copies = pass_on(
+        [
+            same(left.at[c, x, y, big, :], to_y),
+            same(right.at[c, y, x, big, :], to_x),
+            same(left.at[c, x, every, small, cols], to_x),
+            same(right.at[c, y, every, small, cols], to_y),
+        ]
+    )
+    for copy in copies:
+        copy.wait_recv()
+    copies = pass_on(
+        [
+            same(left.at[c, x, every, big, :], to_x),
+            same(right.at[c, y, every, big, :], to_y),
+            same(left.at[c, every, every, small, cols], to_z),
+            same(right.at[c, every, every, small, cols], to_z),
+        ]
+    )
+    across = []
+    for o in range(4):
+        if o > 0:
+            for copy in copies[4 * o - 4 : 4 * o]:
+                copy.wait_recv()
+        from_x, from_y = (x + 4 - o) % 4, (y + 4 - o) % 4
+        from_z = pl.ds(pl.multiple_of(((z + 4 - o) % 4) * 256, 256), 256)
+        for ref in (
+            left.at[c, from_x, every, big, :],
+            right.at[c, from_y, every, big, :],
+            left.at[c, every, every, small, from_z],
+            right.at[c, every, every, small, from_z],
+        ):
+            across.append(ship(ref, ref, other))
+    for copy in across:
+        copy.wait_recv()
+    for copy in started:
+        copy.wait_send()
+
+
+def sketch_rows(scale, signed, coarse, fine):
+    vm = pl.BlockSpec(memory_space=pltpu.VMEM)
+    anywhere = pl.BlockSpec(memory_space=pl.ANY)
+    f32, bf16 = jnp.float32, jnp.bfloat16
+    half = jax.ShapeDtypeStruct((2, 4, 4, 64, D // 2), bf16)
+    left, right = pl.pallas_call(
+        lambda *refs: sketch_kernel(scale, *refs),
+        out_shape=(half, half),
+        in_specs=[vm] * 3,
+        out_specs=(anywhere, anywhere),
+        scratch_shapes=[
+            pltpu.VMEM((4, 256, 512), f32),
+            pltpu.VMEM((4, 256, 512), f32),
+            pltpu.VMEM((4, 256, 512), f32),
+            pltpu.VMEM((2, 4, 256, 256), bf16),
+            pltpu.VMEM((3, 256, 256), bf16),
+            pltpu.VMEM((3, 256, 256), bf16),
+            pltpu.VMEM((2, 4, 64, 256), f32),
+            pltpu.VMEM((3, 64, 256), f32),
+            pltpu.VMEM((3, 64, 256), f32),
+            pltpu.VMEM((2, 64, 256), bf16),
+            pltpu.SemaphoreType.DMA((72,)),
+            pltpu.SemaphoreType.DMA((72,)),
+            pltpu.SemaphoreType.DMA((2,)),
+        ],
+        compiler_params=pltpu.CompilerParams(vmem_limit_bytes=32 * 2**20, collective_id=1, has_side_effects=True),
+        name="sketch",
+    )(signed, coarse, fine)
+    return left.reshape(D, D // 2), right.reshape(D, D // 2)
+
+
 def parity(common):
     for shift in (8, 4, 2, 1):
         common = common ^ (common >> shift)
@@ -329,13 +557,9 @@
     coarse = parity((low[:, None] // 128) & lax.iota(jnp.int32, row_count // 128)[None, :])
     coarse = coarse * parity(high & ex_index)[:, None]
     fine = parity((low[:, None] % 128) & lax.iota(jnp.int32, 128)[None, :])
-    pattern = (coarse.astype(jnp.bfloat16)[:, :, None] * fine.astype(jnp.bfloat16)[:, None, :]).reshape(sample_count, row_count)
-    picked = lax.dot_general(pattern, signed, NN, preferred_element_type=jnp.float32)
-    summed = lax.psum_scatter(picked, "ex", scatter_dimension=0, tiled=True)
-    sketch = (summed * (1.0 / math.sqrt(total_rows * sample_count))).astype(jnp.bfloat16)
-    wide = lax.all_gather(sketch, "feat", axis=1, tiled=True)
-    whole = lax.all_gather(wide, "ex", axis=0, tiled=True)
-    factors = factor(whole)
+    scale = 1.0 / math.sqrt(total_rows * sample_count)
+    left, right = sketch_rows(scale, signed, coarse.astype(jnp.bfloat16), fine.astype(jnp.bfloat16))
+    factors = factor(left, right)
     out = pcg(total_rows, weighted, grad_part[None, :], factors, weights[None, :], radius[None, :])
     return out[0]
 

time: 507 us -> 300 us (0.59)
  waiting for transfers between devices: 135 us -> 0 us
  Pallas kernels: 307 us -> 270 us
  between operations: 14.2 us -> 0.76 us
  blocking collectives: 21.5 us -> 10.7 us
  other arithmetic: 14.5 us -> 6.05 us
  matrix products: 12.1 us -> 4.22 us
  local copies, waits for them, and re-layouts: 2.46 us -> 7.68 us
    pallas_call x1, Pallas kernels: 214 us -> 118 us  [factor(): pl.pallas_call(factor_kernel, out_shape=(jax.ShapeDtypeStruct((D, D), jnp...]
    reduce_scatter x1 -> x0, waiting for transfers between devices: 81.5 us -> none  [local(): summed = lax.psum_scatter(picked, 'ex', scatter_dimension=0, tiled=True)]
    pallas_call x0 -> x1, Pallas kernels: none -> 57.2 us  [sketch_rows(): pl.pallas_call(lambda *refs: sketch_kernel(scale, *refs), out_shape=(half...]
    all_gather x1 -> x0, waiting for transfers between devices: 53.4 us -> none  [local(): whole = lax.all_gather(wide, 'ex', axis=0, tiled=True)]
    all_gather x1 -> x0, blocking collectives: 10.8 us -> none  [local(): wide = lax.all_gather(sketch, 'feat', axis=1, tiled=True)]
    mul x1, other arithmetic: 10.8 us -> 3.25 us  [local(): signed = weighted * signs.astype(jnp.bfloat16)[:, None]]
    dot_general x1 -> x0, matrix products: 6.32 us -> none  [local(): lax.dot_general(pattern, signed, NN, preferred_element_type=jnp.float32)]
    unnamed x11 -> x17, local copies, waits for them, and re-layouts: 2.19 us -> 7.68 us
  transfers between devices with their start and end apart: 2 -> 0, of which waited for: 2 -> 0; matrix products, arithmetic and copies ran while one was open for 0% -> 0% of each run, Pallas kernels for 0% -> 0%
where the time goes in v2:
time: 300 us
  Pallas kernels  270 us (90%)
  blocking collectives  10.7 us (4%)
  local copies, waits for them, and re-layouts  7.68 us (3%)
  other arithmetic  6.05 us (2%)
  matrix products  4.22 us (1%)
    pallas_call x1, Pallas kernels, factor(): pl.pallas_call(factor_kernel, out_shape=(jax.ShapeDtypeStruct((D, D), jnp...  118 us
    pallas_call x1, Pallas kernels, pcg(): pl.pallas_call(lambda *refs: pcg_kernel(total_rows, *refs), out_shape=jax...  94.7 us
    pallas_call x1, Pallas kernels, sketch_rows(): pl.pallas_call(lambda *refs: sketch_kernel(scale, *refs), out_shape=(half...  57.2 us
    psum x1, blocking collectives, local(): margins = lax.psum(jnp.dot(dense, weights, precision=HI), 'feat')  10.7 us
    unnamed x17, local copies, waits for them, and re-layouts  7.68 us

profile of v2, /device:TPU:1, one launch (start us, length us, event | category | flops | bytes accessed | tf_op | source)
XLA Modules:
  0.0 299.6 jit_solution(10396362077064579618)
XLA Ops:
  0.0 0.0 copy-start.6
  0.0 0.7 convert_element_type.21
  0.7 3.3 %fusion.18 = f32[1,2048]{1,0:T(1,128)S(1)} fusion(bf16[2048,512]{1,0:T(8,128)(2,1)} %param.6, f32[512,1]{0,1:T(1,128)} %bitcast.16), kind=kOutput, calls=%fused_computation.47 | convolution fusion | flops 12582912 | bytes 2107392 | tf_op jit(solution)/shard_map/dot_general | solution.py:550
  4.0 10.7 %psum.7 = f32[2048]{0:T(1024)S(1)} all-reduce(f32[2048]{0:T(1024)S(1)} %bitcast.19), channel_id=1, replica_groups=mesh['ex'=32,'feat'=4] {'feat'}, use_global_device_ids=true, to_apply=%region_0.0 | all-reduce | flops 2048 | bytes 16384 | tf_op jit(solution)/shard_map/psum | solution.py:550
  14.7 0.0 copy-done.6
  14.7 0.0 copy-start.5
  14.8 3.2 %broadcast_multiply_fusion = (bf16[2048,512]{1,0:T(8,128)(2,1)}, bf16[2048,512]{1,0:T(8,128)(2,1)S(1)}) fusion(bf16[2048]{0:T(1024)(128)(2,1)S(1)} %convert_element_type.21, bf16[2048,512]{1,0:T(8,128)(2,1)} %param.6, f32[2048]{0:T(1024)S(1)} %get-tuple-element.23), kind=kLoop, calls=%fused_computation.18 | loop fusion | flops 4194304 | bytes 6303744 | tf_op jit(solution)/shard_map/mul | solution.py:555
  18.0 0.0 copy-start.7
  18.0 0.0 copy-done.5
  18.0 0.9 fusion.19.refs_1_
  18.9 0.0 copy-done.7
  19.0 1.4 fusion.4.refs_1_
  20.3 0.7 fusion.8.refs_2_
  21.0 0.0 copy-start
  21.0 1.6 copy-done
  22.6 57.2 %sketch.1 = (bf16[2,4,4,64,1024]{4,3,2,1,0:T(8,128)(2,1)S(1)}, bf16[2,4,4,64,1024]{4,3,2,1,0:T(8,128)(2,1)S(1)}) custom-call(bf16[2048,512]{1,0:T(8,128)(2,1)S(1)} %copy-done, bf16[2048,16]{1,0:T(8,128)(2,1)S(1)} %fusion.4.refs_1_, bf16[2048,128]{1,0:T(8,128)(2,1)S(1)} %fusion.8.refs_2_), custom_call_target="tpu_custom_call" | custom-call | tf_op jit(solution)/shard_map/sketch/pallas_call | solution.py:511
  79.8 0.0 copy-start.1
  79.8 1.9 copy-done.1
  81.8 0.0 copy-start.2
  81.8 2.0 copy-done.2
  83.7 0.0 copy-start.4
  83.7 118.3 %factor.1 = (bf16[2048,2048]{1,0:T(8,128)(2,1)}, bf16[2048,2048]{1,0:T(8,128)(2,1)}, bf16[4,512,512]{2,1,0:T(8,128)(2,1)}, bf16[4,512,512]{2,1,0:T(8,128)(2,1)}) custom-call(bf16[2048,1024]{1,0:T(8,128)(2,1)} %bitcast.14, bf16[2048,1024]{1,0:T(8,128)(2,1)} %bitcast.15), custom_call_target="tpu_custom_call" | custom-call | tf_op jit(solution)/shard_map/factor/pallas_call | solution.py:194
  202.7 0.0 copy-done.4
  202.7 0.0 copy-start.3
  202.7 1.6 copy-done.3
  204.3 94.7 %pcg.1 = f32[1,512]{1,0:T(1,128)S(1)} custom-call(bf16[2048,512]{1,0:T(8,128)(2,1)S(1)} %get-tuple-element.18.refs_0_, f32[1,512]{1,0:T(1,128)S(1)} %fusion.19.refs_1_, bf16[2048,2048]{1,0:T(8,128)(2,1)} %get-tuple-element.13.refs_2_, bf16[2048,2048]{1,0:T(8,128)(2,1)} %get-tuple-element.14.refs_3_, bf16[4,512,512]{2,1,0:T(8,128)(2,1)S(1)} %copy-done.3, ...), custom_call_target="tpu_custom_call" | custom-call | tf_op jit(solution)/shard_map/pcg/pallas_call | solution.py:340
  299.0 0.6 copy.12
  (2 shorter events, 0.1 us)
Async XLA Ops:
  0.0 14.7 %copy-start.6 = (s32[2048]{0:T(1024)S(1)}, s32[2048]{0:T(1024)}, u32[]{:S(2)}) copy-start(s32[2048]{0:T(1024)} %param.8) | copy-start | bytes 24580
  14.7 3.3 %copy-start.5 = (bf16[2048,512]{1,0:T(8,128)(2,1)S(1)}, bf16[2048,512]{1,0:T(8,128)(2,1)}, u32[]{:S(2)}) copy-start(bf16[2048,512]{1,0:T(8,128)(2,1)} %param.6) | copy-start | bytes 6291460
  18.0 0.9 copy-start.7
  21.0 1.6 copy-start
  79.8 1.9 copy-start.1
  81.8 2.0 copy-start.2
  83.7 119.0 %copy-start.4 = (f32[512]{0:T(512)S(1)}, f32[512]{0:T(512)}, u32[]{:S(2)}) copy-start(f32[512]{0:T(512)} %param.7) | copy-start | bytes 6148
  202.7 1.6 copy-start.3

commit v3 on v2

--- a/solution.py
+++ b/solution.py
@@ -102,7 +102,7 @@
     return lower * (1.0 / along_rows) * (1.0 / jnp.sqrt(along_cols))
 
 
-def factor_kernel(left, right, up_hi, up_lo, inv_hi, inv_lo, gram, invs, trio_l, trio_r):
+def factor_kernel(left, right, up_hi, up_lo, inv_hi, inv_lo, gram, invs, crosses, corner, trio_l, trio_r):
     ridge = REG / D
     halves = (left, right)
     for a in range(4):
@@ -123,67 +123,83 @@
                     if a == b and h < side:
                         gram[512 * a + 256 : 512 * a + 512, 512 * a : 512 * a + 256] = jnp.zeros((256, 256), jnp.float32)
 
-    def step(k, carry):
-        at = pl.multiple_of(k * 128, 128)
-        rows = pl.ds(at, 128)
-        inverse = block_inverse(gram[rows, rows])
-        invs[k] = inverse
-        first = k // 4
+    def join(top, bottom, cross):
+        middle = lax.dot_general(cross, top, TN, precision=HI, preferred_element_type=jnp.float32)
+        edge = -lax.dot_general(bottom, middle, NN, precision=HI, preferred_element_type=jnp.float32)
+        zero = jnp.zeros_like(top)
+        return jnp.concatenate([jnp.concatenate([top, zero], axis=1), jnp.concatenate([edge, bottom], axis=1)], axis=0)
+
+    def step(s, carry):
+        at = pl.multiple_of(s * 256, 256)
+        next_at = pl.multiple_of(at + 128, 128)
+        rows = pl.ds(at, 256)
+        first = s // 2
+        upper, lower = pl.ds(at, 128), pl.ds(next_at, 128)
+        corner[0] = gram[upper, upper]
+
+        def one(h, carry):
+            corner[2 + h] = block_inverse(corner[h])
+
+            if h == 0:
+                cross = lax.dot_general(corner[2], gram[upper, lower], NN, precision=HI, preferred_element_type=jnp.float32)
+                corner[4] = cross
+                corner[1] = gram[lower, lower] - lax.dot_general(cross, cross, TN, precision=HI, preferred_element_type=jnp.float32)
+
+            return carry
+
+        one(0, 0)
+        one(1, 0)
+        inverse = join(corner[2], corner[3], corner[4])
+        invs[s] = inverse
         ih, il = split2(inverse)
         ileft = jnp.concatenate([ih, ih, il], axis=1)
+        half = pl.ds(pl.multiple_of((s % 2) * 256, 256), 256)
         for c in range(4):
 
-            @pl.when(c >= first)
+            @pl.when(c >= (s + 1) // 2)
             def _():
                 cs = slice(512 * c, 512 * c + 512)
                 gh, gl = split2(gram[rows, cs])
                 panel = lax.dot_general(ileft, jnp.concatenate([gh, gl, gh], axis=0), NN, preferred_element_type=jnp.float32)
-                cols = lax.broadcasted_iota(jnp.int32, (128, 512), 1) + 512 * c
-                panel = jnp.where(cols >= at + 128, panel, 0.0)
-                gram[rows, cs] = panel
+                cols = lax.broadcasted_iota(jnp.int32, (256, 512), 1) + 512 * c
+                panel = jnp.where(cols >= at + 256, panel, 0.0)
                 ph, plo = split2(panel)
-                trio_r[0:128, cs] = ph
-                trio_r[128:256, cs] = plo
-                trio_r[256:384, cs] = ph
-                trio_l[0:128, cs] = ph
-                trio_l[128:256, cs] = ph
-                trio_l[256:384, cs] = plo
-
-        for a in range(4):
-
-            @pl.when(a >= first)
-            def _():
-                ra = slice(512 * a, 512 * a + 512)
-                for b in range(a, 4):
-                    cs = slice(512 * b, 512 * b + 512)
-                    gram[ra, cs] = gram[ra, cs] - lax.dot_general(trio_l[:, ra], trio_r[:, cs], TN, preferred_element_type=jnp.float32)
-
+                trio_r[0:256, cs] = ph
+                trio_r[256:512, cs] = plo
+                trio_r[512:768, cs] = ph
+                trio_l[0:256, cs] = ph
+                trio_l[256:512, cs] = ph
+                trio_l[512:768, cs] = plo
+
+                @pl.when(c == first)
+                def _():
+                    crosses[first] = panel[:, 256:]
+
+                @pl.when(c > first)
+                def _():
+                    block = first * (7 - first) // 2 + c - first - 1
+                    up_hi[block, half, :] = ph
+                    up_lo[block, half, :] = plo
+
+        def across(a, carry):
+            ra = pl.ds(pl.multiple_of(a * 512, 512), 512)
+
+            def along(b, carry):
+                cs = pl.ds(pl.multiple_of(b * 512, 512), 512)
+                gram[ra, cs] = gram[ra, cs] - lax.dot_general(trio_l[:, ra], trio_r[:, cs], TN, preferred_element_type=jnp.float32)
+                return carry
+
+            return lax.fori_loop(a, 4, along, carry)
+
+        lax.fori_loop((s + 1) // 2, 4, across, 0)
         return carry
 
-    lax.fori_loop(0, 16, step, 0)
+    lax.fori_loop(0, 8, step, 0)
 
     def chunk(a, carry):
-        at = pl.multiple_of(a * 512, 512)
-
-        def up(i, j, size):
-            return gram[pl.ds(pl.multiple_of(at + i, 128), size), pl.ds(pl.multiple_of(at + j, 128), size)]
-
-        def join(top, bottom, cross):
-            middle = lax.dot_general(cross, top, TN, precision=HI, preferred_element_type=jnp.float32)
-            corner = -lax.dot_general(bottom, middle, NN, precision=HI, preferred_element_type=jnp.float32)
-            zero = jnp.zeros_like(top)
-            return jnp.concatenate([jnp.concatenate([top, zero], axis=1), jnp.concatenate([corner, bottom], axis=1)], axis=0)
-
-        q = [invs[4 * a + i] for i in range(4)]
-        one = join(q[0], q[1], up(0, 128, 128))
-        two = join(q[2], q[3], up(256, 384, 128))
-        whole = join(one, two, up(0, 256, 256))
-        hi, lo = split2(whole)
+        hi, lo = split2(join(invs[2 * a], invs[2 * a + 1], crosses[a]))
         inv_hi[a] = hi
         inv_lo[a] = lo
-        hi, lo = split2(gram[pl.ds(at, 512), :])
-        up_hi[pl.ds(at, 512), :] = hi
-        up_lo[pl.ds(at, 512), :] = lo
         return carry
 
     lax.fori_loop(0, 4, chunk, 0)
@@ -191,23 +207,23 @@
 
 def factor(left, right):
     vm = pl.BlockSpec(memory_space=pltpu.VMEM)
+    ups = jax.ShapeDtypeStruct((6, 512, 512), jnp.bfloat16)
+    inverses = jax.ShapeDtypeStruct((4, 512, 512), jnp.bfloat16)
     return pl.pallas_call(
         factor_kernel,
-        out_shape=(
-            jax.ShapeDtypeStruct((D, D), jnp.bfloat16),
-            jax.ShapeDtypeStruct((D, D), jnp.bfloat16),
-            jax.ShapeDtypeStruct((4, 512, 512), jnp.bfloat16),
-            jax.ShapeDtypeStruct((4, 512, 512), jnp.bfloat16),
-        ),
+        out_shape=(ups, ups, inverses, inverses),
         in_specs=[vm, vm],
         out_specs=(vm, vm, vm, vm),
         scratch_shapes=[
             pltpu.VMEM((D, D), jnp.float32),
-            pltpu.VMEM((16, 128, 128), jnp.float32),
-            pltpu.VMEM((384, D), jnp.bfloat16),
-            pltpu.VMEM((384, D), jnp.bfloat16),
+            pltpu.VMEM((8, 256, 256), jnp.float32),
+            pltpu.VMEM((4, 256, 256), jnp.float32),
+            pltpu.VMEM((5, 128, 128), jnp.float32),
+            pltpu.VMEM((768, D), jnp.bfloat16),
+            pltpu.VMEM((768, D), jnp.bfloat16),
         ],
-        compiler_params=pltpu.CompilerParams(vmem_limit_bytes=60 * 2**20),
+        compiler_params=pltpu.CompilerParams(vmem_limit_bytes=50 * 2**20),
+        cost_estimate=pl.CostEstimate(flops=60 * 10**9, bytes_accessed=18 * 2**20, transcendentals=0),
         name="factor",
     )(left, right)
 
@@ -222,16 +238,25 @@
     return stacked.astype(jnp.bfloat16)
 
 
-def row_times(row, matrix, dims):
-    return jnp.sum(lax.dot_general(pieces(row), matrix, dims, preferred_element_type=jnp.float32), axis=0, keepdims=True)
-
-
-def pcg_kernel(total_rows, weighted, grad, up_hi, up_lo, inv_hi, inv_lo, weights, radius, out, full, zbuf, abuf, bbuf, zs, zr, a_s, a_r, b_s, b_r):
+def pair(row):
+    first = row.astype(jnp.bfloat16).astype(jnp.float32)
+    which = lax.broadcasted_iota(jnp.int32, (16, row.shape[1]), 0)
+    return jnp.where(which == 0, first, jnp.where(which == 1, row - first, 0.0)).astype(jnp.bfloat16)
+
+
+def place(a, b):
+    return a * (7 - a) // 2 + b - a - 1
+
+
+def pcg_kernel(total_rows, w0, w1, w2, w3, grad, up_hi, up_lo, inv_hi, inv_lo, weights, radius, out, full, wide, abuf, bbuf, a_s, a_r, b_s, b_r):
     ex = lax.axis_index("ex")
     feat = lax.axis_index("feat")
     plane, within = ex // 8, ex % 8
     ridge = REG / D
-    own = pl.ds(pl.multiple_of(feat * 512, 512), 512)
+    blocks = (w0, w1, w2, w3)
+
+    def columns(o):
+        return pl.ds(pl.multiple_of(((feat + 4 - o) % 4) * 512, 512), 512)
 
     def near(o):
         return (plane * 8 + (within + o) % 8, feat)
@@ -239,9 +264,6 @@
     def far(o):
         other = (plane * 4 + feat + o) % 16
         return ((other // 4) * 8 + within, other % 4)
-
-    def along(o):
-        return (ex, (feat + o) % 4)
 
     barrier = pltpu.get_barrier_semaphore()
     for o in range(1, 8):
@@ -267,53 +289,41 @@
             copy.start()
         for copy in copies:
             copy.wait()
-
-    def over_examples(part, turn):
-        exchange(part, abuf, turn, within, 8, near, a_s, a_r)
-        total = abuf[turn, 0]
-        for q in range(1, 8):
-            total = total + abuf[turn, q]
-        exchange(total, bbuf, turn, plane * 4 + feat, 16, far, b_s, b_r)
-        parts = []
-        for z in range(4):
-            parts.append((bbuf[turn, z] + bbuf[turn, 4 + z]) + (bbuf[turn, 8 + z] + bbuf[turn, 12 + z]))
-        return jnp.concatenate(parts, axis=1)
-
-    def over_features(part, turn):
-        exchange(part, zbuf, turn, feat, 4, along, zs, zr)
-        return (zbuf[turn, 0] + zbuf[turn, 1]) + (zbuf[turn, 2] + zbuf[turn, 3])
-
-    def times(row, high, low, dims):
-        high_row = row.astype(jnp.bfloat16).astype(jnp.float32)
-        which = lax.broadcasted_iota(jnp.int32, (16, row.shape[1]), 0)
-        stacked = jnp.where(which == 0, high_row, jnp.where(which == 1, row - high_row, 0.0)).astype(jnp.bfloat16)
-        product = lax.dot_general(stacked, high, dims, preferred_element_type=jnp.float32)
-        product = product + lax.dot_general(stacked, low, dims, preferred_element_type=jnp.float32)
-        return jnp.sum(product, axis=0, keepdims=True)
+        totals = [buf[turn, q] for q in range(count)]
+        while len(totals) > 1:
+            totals = [totals[i] + totals[i + 1] for i in range(0, len(totals), 2)]
+        return totals[0]
+
+    def everywhere(part, turn):
+        return exchange(exchange(part, abuf, turn, within, 8, near, a_s, a_r), bbuf, turn, plane * 4 + feat, 16, far, b_s, b_r)
+
+    def product(stacked, high, low, dims):
+        total = lax.dot_general(stacked, high, dims, preferred_element_type=jnp.float32)
+        total = total + lax.dot_general(stacked, low, dims, preferred_element_type=jnp.float32)
+        return jnp.sum(total, axis=0, keepdims=True)
 
     def solve(row):
-        rest = row
-        middle = []
+        rest = [row[:, 512 * a : 512 * a + 512] for a in range(4)]
         for a in range(4):
-            part = times(rest[:, :512], inv_hi[a], inv_lo[a], NT)
-            middle.append(part)
-            if a < 3:
-                here, right = slice(512 * a, 512 * a + 512), slice(512 * a + 512, D)
-                rest = rest[:, 512:] - times(part, up_hi[here, right], up_lo[here, right], NN)
-        rest = jnp.concatenate(middle, axis=1)
-        result = []
+            rest[a] = product(pair(rest[a]), inv_hi[a], inv_lo[a], NT)
+            stacked = pair(rest[a])
+            for b in range(a + 1, 4):
+                at = place(a, b)
+                rest[b] = rest[b] - product(stacked, up_hi[at], up_lo[at], NN)
         for a in range(3, -1, -1):
-            part = times(rest[:, 512 * a :], inv_hi[a], inv_lo[a], NN)
-            result.insert(0, part)
-            if a > 0:
-                above, here = slice(0, 512 * a), slice(512 * a, 512 * a + 512)
-                rest = rest[:, : 512 * a] - times(part, up_hi[above, here], up_lo[above, here], NT)
-        return jnp.concatenate(result, axis=1)
+            rest[a] = product(pair(rest[a]), inv_hi[a], inv_lo[a], NN)
+            stacked = pair(rest[a])
+            for b in range(a):
+                at = place(b, a)
+                rest[b] = rest[b] - product(stacked, up_hi[at], up_lo[at], NT)
+        return jnp.concatenate(rest, axis=1)
 
     def dot(left, right):
         return jnp.sum(left * right, axis=1, keepdims=True)
 
-    residual = -over_examples(grad[...] * (1.0 / total_rows) + weights[...] * (ridge / 32), 0)
+    wide[...] = jnp.zeros((1, D), jnp.float32)
+    wide[:, columns(0)] = grad[...] * (1.0 / total_rows) + weights[...] * (ridge / 32)
+    residual = -everywhere(wide[...], 0)
 
     def step(number, carry):
         answer, residual, direction, inner = carry
@@ -321,9 +331,14 @@
         inner_now = dot(residual, solved)
         direction = solved + jnp.where(number == 0, 0.0, inner_now / inner) * direction
         full[...] = direction
-        row_sums = over_features(row_times(full[:, own], weighted[...], NT), number)
-        product = over_examples(row_times(row_sums, weighted[...], NN), number + 1)
-        curved = product * (1.0 / total_rows) + ridge * direction
+        row_sums = jnp.zeros((16, 512), jnp.float32)
+        for o in range(4):
+            row_sums = row_sums + lax.dot_general(pieces(full[:, columns(o)]), blocks[o][...], NT, preferred_element_type=jnp.float32)
+        stacked = pieces(jnp.sum(row_sums, axis=0, keepdims=True))
+        for o in range(4):
+            part = lax.dot_general(stacked, blocks[o][...], NN, preferred_element_type=jnp.float32)
+            wide[:, columns(o)] = jnp.sum(part, axis=0, keepdims=True)
+        curved = everywhere(wide[...], number + 1) * (1.0 / total_rows) + ridge * direction
         step_size = inner_now / dot(direction, curved)
         return answer + step_size * direction, residual - step_size * curved, direction, inner_now
 
@@ -331,32 +346,30 @@
     answer = lax.fori_loop(0, ITERS, step, (zero, residual, zero, jnp.ones((1, 1), jnp.float32)))[0]
     scale = jnp.minimum(1.0, radius[...] * math.sqrt(D) / jnp.sqrt(dot(answer, answer) + 1e-06))
     full[...] = answer
-    out[...] = weights[...] + scale * full[:, own]
-
-
-def pcg(total_rows, weighted, grad, factors, weights, radius):
+    out[...] = weights[...] + scale * full[:, columns(0)]
+
+
+def pcg(total_rows, blocks, grad, factors, weights, radius):
     vm = pl.BlockSpec(memory_space=pltpu.VMEM)
     dma = pltpu.SemaphoreType.DMA
     return pl.pallas_call(
         lambda *refs: pcg_kernel(total_rows, *refs),
         out_shape=jax.ShapeDtypeStruct((1, 512), jnp.float32),
-        in_specs=[vm] * 8,
+        in_specs=[vm] * 11,
         out_specs=vm,
         scratch_shapes=[
             pltpu.VMEM((1, D), jnp.float32),
-            pltpu.VMEM((4, 4, 1, D), jnp.float32),
-            pltpu.VMEM((5, 8, 1, 512), jnp.float32),
-            pltpu.VMEM((5, 16, 1, 512), jnp.float32),
-            dma((4, 4)),
-            dma((4, 4)),
+            pltpu.VMEM((1, D), jnp.float32),
+            pltpu.VMEM((5, 8, 1, D), jnp.float32),
+            pltpu.VMEM((5, 16, 1, D), jnp.float32),
             dma((5, 8)),
             dma((5, 8)),
             dma((5, 16)),
             dma((5, 16)),
         ],
-        compiler_params=pltpu.CompilerParams(vmem_limit_bytes=48 * 2**20, collective_id=0, has_side_effects=True),
+        compiler_params=pltpu.CompilerParams(vmem_limit_bytes=32 * 2**20, collective_id=0, has_side_effects=True),
         name="pcg",
-    )(weighted, grad, *factors, weights, radius)
+    )(*blocks, grad, *factors, weights, radius)
 
 
 def sketch_kernel(scale, signed, coarse, fine, left, right, send, keep, arrive, narrow, xin, yin, stage, xlast, ylast, mine, ssem, rsem, lsem):
@@ -560,7 +573,13 @@
     scale = 1.0 / math.sqrt(total_rows * sample_count)
     left, right = sketch_rows(scale, signed, coarse.astype(jnp.bfloat16), fine.astype(jnp.bfloat16))
     factors = factor(left, right)
-    out = pcg(total_rows, weighted, grad_part[None, :], factors, weights[None, :], radius[None, :])
+    feat_index = lax.axis_index("feat")
+    part = row_count // 4
+    blocks = []
+    for o in range(4):
+        rows = lax.dynamic_slice_in_dim(weighted, ((feat_index + o) % 4) * part, part, 0)
+        blocks.append(lax.ppermute(rows, "feat", [(i, (i + o) % 4) for i in range(4)]) if o else rows)
+    out = pcg(total_rows, blocks, grad_part[None, :], factors, weights[None, :], radius[None, :])
     return out[0]
 
 

time: 300 us -> 274 us (0.913)
  Pallas kernels: 270 us -> 238 us
  local copies, waits for them, and re-layouts: 7.68 us -> 11 us
    pallas_call x1, Pallas kernels: 118 us -> 99.3 us  [factor(): pl.pallas_call(factor_kernel, out_shape=(ups, ups, inverses, inverses), i...]
    pallas_call x1, Pallas kernels: 94.7 us -> 78.1 us  [pcg(): pl.pallas_call(lambda *refs: pcg_kernel(total_rows, *refs), out_shape=jax...]
    pallas_call x1, Pallas kernels: 57.2 us -> 60.6 us  [sketch_rows(): pl.pallas_call(lambda *refs: sketch_kernel(scale, *refs), out_shape=(half...]
    unnamed x17 -> x19, local copies, waits for them, and re-layouts: 7.68 us -> 8.28 us
  transfers between devices with their start and end apart: 0 -> 3, of which waited for: 0 -> 0; matrix products, arithmetic and copies ran while one was open for 0% -> 1% of each run, Pallas kernels for 0% -> 58%
where the time goes in v3:
time: 274 us; the launch traced here: 273 us
  Pallas kernels  238 us (87%)
  local copies, waits for them, and re-layouts  11 us (4%)
  blocking collectives  10.7 us (4%)
  other arithmetic  5.85 us (2%)
  matrix products  4.22 us (2%)
    pallas_call x1, Pallas kernels, factor(): pl.pallas_call(factor_kernel, out_shape=(ups, ups, inverses, inverses), i...  99.3 us
    pallas_call x1, Pallas kernels, pcg(): pl.pallas_call(lambda *refs: pcg_kernel(total_rows, *refs), out_shape=jax...  78.1 us
    pallas_call x1, Pallas kernels, sketch_rows(): pl.pallas_call(lambda *refs: sketch_kernel(scale, *refs), out_shape=(half...  60.6 us
    psum x1, blocking collectives, local(): margins = lax.psum(jnp.dot(dense, weights, precision=HI), 'feat')  10.7 us
    unnamed x19, local copies, waits for them, and re-layouts  8.28 us
  transfers between devices with their start and end apart: 3, of which 0 were waited for; matrix products, arithmetic and copies ran while one was open for 1% of the time, Pallas kernels for 58%

profile of v3, /device:TPU:1, one launch (start us, length us, event | category | flops | bytes accessed | tf_op | source)
XLA Modules:
  0.0 273.3 jit_solution(2888142494364504032)
XLA Ops:
  0.0 0.0 copy-start.7
  0.0 0.7 convert_element_type.21
  0.7 3.3 %fusion.18 = f32[1,2048]{1,0:T(1,128)S(1)} fusion(bf16[2048,512]{1,0:T(8,128)(2,1)} %param.6, f32[512,1]{0,1:T(1,128)} %bitcast.14), kind=kOutput, calls=%fused_computation.51 | convolution fusion | flops 12582912 | bytes 2107392 | tf_op jit(solution)/shard_map/dot_general | solution.py:563
  4.0 10.7 %psum.7 = f32[2048]{0:T(1024)S(1)} all-reduce(f32[2048]{0:T(1024)S(1)} %bitcast.19), channel_id=1, replica_groups=mesh['ex'=32,'feat'=4] {'feat'}, use_global_device_ids=true, to_apply=%region_0.0 | all-reduce | flops 2048 | bytes 16384 | tf_op jit(solution)/shard_map/psum | solution.py:563
  14.7 0.0 copy-done.7
  14.7 3.1 %broadcast_multiply_fusion = (bf16[2048,512]{1,0:T(8,128)(2,1)S(1)}, bf16[2048,512]{1,0:T(8,128)(2,1)}) fusion(bf16[2048]{0:T(1024)(128)(2,1)S(1)} %convert_element_type.21, bf16[2048,512]{1,0:T(8,128)(2,1)} %param.6, f32[2048]{0:T(1024)S(1)} %get-tuple-element.27), kind=kLoop, calls=%fused_computation.18 | loop fusion | flops 4194304 | bytes 6303744 | tf_op jit(solution)/shard_map/mul | solution.py:568
  17.8 0.0 copy-start.8
  17.8 2.7 constant_dynamic-slice_fusion
  20.5 0.0 collective-permute-start
  20.5 0.9 collective-permute-start.1
  21.5 1.7 collective-permute-start.2
  23.2 0.0 copy-done.8
  23.2 0.7 fusion.8.refs_2_
  23.9 1.4 fusion.4.refs_1_
  25.3 60.6 %sketch.1 = (bf16[2,4,4,64,1024]{4,3,2,1,0:T(8,128)(2,1)S(1)}, bf16[2,4,4,64,1024]{4,3,2,1,0:T(8,128)(2,1)S(1)}) custom-call(bf16[2048,512]{1,0:T(8,128)(2,1)S(1)} %get-tuple-element.17.refs_0_, bf16[2048,16]{1,0:T(8,128)(2,1)S(1)} %fusion.4.refs_1_, bf16[2048,128]{1,0:T(8,128)(2,1)S(1)} %fusion.8.refs_2_), custom_call_target="tpu_custom_call" | custom-call | tf_op jit(solution)/shard_map/sketch/pallas_call | solution.py:524
  85.9 0.0 copy-start.4
  85.9 1.9 copy-done.4
  87.8 0.0 copy-start.5
  87.8 2.0 copy-done.5
  89.8 99.3 %factor.1 = (bf16[6,512,512]{2,1,0:T(8,128)(2,1)}, bf16[6,512,512]{2,1,0:T(8,128)(2,1)}, bf16[4,512,512]{2,1,0:T(8,128)(2,1)S(1)}, bf16[4,512,512]{2,1,0:T(8,128)(2,1)}) custom-call(bf16[2048,1024]{1,0:T(8,128)(2,1)} %bitcast.17, bf16[2048,1024]{1,0:T(8,128)(2,1)} %bitcast.18), custom_call_target="tpu_custom_call" | custom-call | flops 60000002048 | bytes 18874368 | tf_op jit(solution)/shard_map/factor/pallas_call | solution.py:212
  189.9 0.0 copy-done.6
  189.9 0.9 fusion.19.refs_4_
  190.8 0.0 collective-permute-done.refs_1_
  190.8 0.0 collective-permute-done.1.refs_2_
  190.8 0.0 collective-permute-done.2.refs_3_
  190.8 0.0 copy-done.2
  190.8 0.0 copy-done.3
  190.8 0.0 copy-start
  190.8 1.9 copy-done
  192.7 1.9 copy-done.1
  194.6 78.1 %pcg.1 = f32[1,512]{1,0:T(1,128)S(1)} custom-call(bf16[512,512]{1,0:T(8,128)(2,1)S(1)} %get-tuple-element.22.refs_0_, bf16[512,512]{1,0:T(8,128)(2,1)S(1)} %collective-permute-done.refs_1_, bf16[512,512]{1,0:T(8,128)(2,1)} %collective-permute-done.1.refs_2_, bf16[512,512]{1,0:T(8,128)(2,1)} %collective-permute-done.2.refs_3_, f32[1,512]{1,0:T(1,128)S(1)} %fusion.19.refs_4_, ...), custom_call_target="tpu_custom_call" | custom-call | tf_op jit(solution)/shard_map/pcg/pallas_call | solution.py:355
  272.7 0.6 copy.13
  (6 shorter events, 0.0 us)
Async XLA Ops:
  0.0 14.7 %copy-start.7 = (s32[2048]{0:T(1024)S(1)}, s32[2048]{0:T(1024)}, u32[]{:S(2)}) copy-start(s32[2048]{0:T(1024)} %param.8) | copy-start | bytes 24580
  17.8 5.4 %copy-start.8 = (s32[2048]{0:T(1024)S(1)}, s32[2048]{0:T(1024)}, u32[]{:S(2)}) copy-start(s32[2048]{0:T(1024)} %param.10) | copy-start | bytes 24580
  20.5 170.3 %collective-permute-start = (bf16[512,512]{1,0:T(8,128)(2,1)}, bf16[512,512]{1,0:T(8,128)(2,1)S(1)}, u32[]{:S(2)}, u32[]{:S(2)}) collective-permute-start(bf16[512,512]{1,0:T(8,128)(2,1)} %get-tuple-element.21), channel_id=1, source_target_pairs={{0,1},{1,2},{2,3},{3,0},{4,5},{5,6},{6,7},{7,4},{8,9},{9,10},{10,1... | collective-permute-start | bytes 1572872 | tf_op jit(solution)/shard_map/ppermute | solution.py:581
  20.5 170.3 %collective-permute-start.1 = (bf16[512,512]{1,0:T(8,128)(2,1)}, bf16[512,512]{1,0:T(8,128)(2,1)}, u32[]{:S(2)}, u32[]{:S(2)}) collective-permute-start(bf16[512,512]{1,0:T(8,128)(2,1)} %get-tuple-element.20), channel_id=1, source_target_pairs={{0,2},{1,3},{2,0},{3,1},{4,6},{5,7},{6,4},{7,5},{8,10},{9,11},{10,... | collective-permute-start | bytes 1572872 | tf_op jit(solution)/shard_map/ppermute | solution.py:581
  21.5 169.3 %collective-permute-start.2 = (bf16[512,512]{1,0:T(8,128)(2,1)}, bf16[512,512]{1,0:T(8,128)(2,1)}, u32[]{:S(2)}, u32[]{:S(2)}) collective-permute-start(bf16[512,512]{1,0:T(8,128)(2,1)} %get-tuple-element.19), channel_id=1, source_target_pairs={{0,3},{1,0},{2,1},{3,2},{4,7},{5,4},{6,5},{7,6},{8,11},{9,8},{10,9... | collective-permute-start | bytes 1572872 | tf_op jit(solution)/shard_map/ppermute | solution.py:581
  85.9 2.0 copy-start.4
  87.8 2.0 copy-start.5
  89.8 100.1 %copy-start.6 = (bf16[2048,512]{1,0:T(8,128)(2,1)S(1)}, bf16[2048,512]{1,0:T(8,128)(2,1)}, u32[]{:S(2)}) copy-start(bf16[2048,512]{1,0:T(8,128)(2,1)} %param.6) | copy-start | bytes 6291460
  189.1 1.8 copy-start.2
  189.1 1.8 copy-start.3
  190.8 1.9 copy-start
  192.7 1.9 copy-start.1

commit v4 on v3

--- a/solution.py
+++ b/solution.py
@@ -222,7 +222,7 @@
             pltpu.VMEM((768, D), jnp.bfloat16),
             pltpu.VMEM((768, D), jnp.bfloat16),
         ],
-        compiler_params=pltpu.CompilerParams(vmem_limit_bytes=50 * 2**20),
+        compiler_params=pltpu.CompilerParams(vmem_limit_bytes=30 * 2**20),
         cost_estimate=pl.CostEstimate(flops=60 * 10**9, bytes_accessed=18 * 2**20, transcendentals=0),
         name="factor",
     )(left, right)
@@ -248,12 +248,11 @@
     return a * (7 - a) // 2 + b - a - 1
 
 
-def pcg_kernel(total_rows, w0, w1, w2, w3, grad, up_hi, up_lo, inv_hi, inv_lo, weights, radius, out, full, wide, abuf, bbuf, a_s, a_r, b_s, b_r):
+def pcg_kernel(total_rows, blocks, start, up_hi, up_lo, inv_hi, inv_lo, weights, radius, out, full, wide, abuf, bbuf, a_s, a_r, b_s, b_r):
     ex = lax.axis_index("ex")
     feat = lax.axis_index("feat")
     plane, within = ex // 8, ex % 8
     ridge = REG / D
-    blocks = (w0, w1, w2, w3)
 
     def columns(o):
         return pl.ds(pl.multiple_of(((feat + 4 - o) % 4) * 512, 512), 512)
@@ -321,9 +320,7 @@
     def dot(left, right):
         return jnp.sum(left * right, axis=1, keepdims=True)
 
-    wide[...] = jnp.zeros((1, D), jnp.float32)
-    wide[:, columns(0)] = grad[...] * (1.0 / total_rows) + weights[...] * (ridge / 32)
-    residual = -everywhere(wide[...], 0)
+    residual = start[...]
 
     def step(number, carry):
         answer, residual, direction, inner = carry
@@ -333,12 +330,12 @@
         full[...] = direction
         row_sums = jnp.zeros((16, 512), jnp.float32)
         for o in range(4):
-            row_sums = row_sums + lax.dot_general(pieces(full[:, columns(o)]), blocks[o][...], NT, preferred_element_type=jnp.float32)
+            row_sums = row_sums + lax.dot_general(pieces(full[:, columns(o)]), blocks[o], NT, preferred_element_type=jnp.float32)
         stacked = pieces(jnp.sum(row_sums, axis=0, keepdims=True))
         for o in range(4):
-            part = lax.dot_general(stacked, blocks[o][...], NN, preferred_element_type=jnp.float32)
+            part = lax.dot_general(stacked, blocks[o], NN, preferred_element_type=jnp.float32)
             wide[:, columns(o)] = jnp.sum(part, axis=0, keepdims=True)
-        curved = everywhere(wide[...], number + 1) * (1.0 / total_rows) + ridge * direction
+        curved = everywhere(wide[...], number) * (1.0 / total_rows) + ridge * direction
         step_size = inner_now / dot(direction, curved)
         return answer + step_size * direction, residual - step_size * curved, direction, inner_now
 
@@ -349,30 +346,37 @@
     out[...] = weights[...] + scale * full[:, columns(0)]
 
 
-def pcg(total_rows, blocks, grad, factors, weights, radius):
+def pcg(total_rows, blocks, start, factors, weights, radius):
     vm = pl.BlockSpec(memory_space=pltpu.VMEM)
     dma = pltpu.SemaphoreType.DMA
     return pl.pallas_call(
         lambda *refs: pcg_kernel(total_rows, *refs),
         out_shape=jax.ShapeDtypeStruct((1, 512), jnp.float32),
-        in_specs=[vm] * 11,
+        in_specs=[vm] * 8,
         out_specs=vm,
         scratch_shapes=[
             pltpu.VMEM((1, D), jnp.float32),
             pltpu.VMEM((1, D), jnp.float32),
-            pltpu.VMEM((5, 8, 1, D), jnp.float32),
-            pltpu.VMEM((5, 16, 1, D), jnp.float32),
-            dma((5, 8)),
-            dma((5, 8)),
-            dma((5, 16)),
-            dma((5, 16)),
+            pltpu.VMEM((4, 8, 1, D), jnp.float32),
+            pltpu.VMEM((4, 16, 1, D), jnp.float32),
+            dma((4, 8)),
+            dma((4, 8)),
+            dma((4, 16)),
+            dma((4, 16)),
         ],
         compiler_params=pltpu.CompilerParams(vmem_limit_bytes=32 * 2**20, collective_id=0, has_side_effects=True),
         name="pcg",
-    )(*blocks, grad, *factors, weights, radius)
-
-
-def sketch_kernel(scale, signed, coarse, fine, left, right, send, keep, arrive, narrow, xin, yin, stage, xlast, ylast, mine, ssem, rsem, lsem):
+    )(blocks, start, *factors, weights, radius)
+
+
+def row_times(row, matrix, dims):
+    return jnp.sum(lax.dot_general(pieces(row), matrix, dims, preferred_element_type=jnp.float32), axis=0, keepdims=True)
+
+def sketch_kernel(
+    scale, total_rows, features, weights, labels, signs, coarse, fine,
+    left, right, residual, blocks,
+    send, keep, arrive, narrow, xin, yin, stage, xlast, ylast, mine, pattern, weighted, wide, zbuf, abuf, bbuf, ssem, rsem, lsem,
+):
     ex = lax.axis_index("ex")
     z = lax.axis_index("feat")
     y, x, c = ex // 8, (ex // 2) % 4, ex % 2
@@ -387,11 +391,20 @@
         return (ex, (z + o) % 4)
 
     other = (ex + 1 - 2 * c, z)
+    within = ex % 8
+
+    def near(o):
+        return (y * 8 + (within + o) % 8, z)
+
+    def far(o):
+        to = (y * 4 + z + o) % 16
+        return ((to // 4) * 8 + within, to % 4)
+
     barrier = pltpu.get_barrier_semaphore()
-    for o in range(1, 4):
-        for peer in (to_x, to_y, to_z):
-            pl.semaphore_signal(barrier, inc=1, device_id=peer(o), device_id_type=MESH)
-    pl.semaphore_signal(barrier, inc=1, device_id=other, device_id_type=MESH)
+    for o in range(1, 8):
+        pl.semaphore_signal(barrier, inc=1, device_id=near(o), device_id_type=MESH)
+    for o in range(1, 16):
+        pl.semaphore_signal(barrier, inc=1, device_id=far(o), device_id_type=MESH)
 
     started = []
 
@@ -404,18 +417,59 @@
         started.append(copy)
         return copy
 
+    def spread(buf, me, count, peer):
+        return [ship(buf.at[me], buf.at[me], peer(o)) for o in range(1, count)]
+
+    def gathered(copies, buf, count):
+        for copy in copies:
+            copy.wait_recv()
+        totals = [buf[q] for q in range(count)]
+        while len(totals) > 1:
+            totals = [totals[i] + totals[i + 1] for i in range(0, len(totals), 2)]
+        return totals[0]
+
+    zbuf[z] = row_times(weights[...], features[...], NT)
+    pl.semaphore_wait(barrier, 22)
+    margin_copies = spread(zbuf, z, 4, to_z)
+    sign_row = signs[...].astype(jnp.bfloat16)
+
+    def patterns(q, carry):
+        rows = pl.ds(pl.multiple_of(q * 256, 256), 256)
+        fine_rows = fine[rows, :]
+        for h in range(16):
+            signed_rows = fine_rows * jnp.broadcast_to(sign_row[:, 128 * h : 128 * h + 128], (256, 128))
+            pattern[rows, 128 * h : 128 * h + 128] = signed_rows * jnp.broadcast_to(coarse[rows, h : h + 1], (256, 128))
+        return carry
+
+    lax.fori_loop(0, 8, patterns, 0)
+    margins = gathered(margin_copies, zbuf, 4)
+    probability = 1.0 / (1.0 + jnp.exp(-margins))
+    root = jnp.sqrt(probability * (1.0 - probability))
+    for i in range(16):
+        rows = slice(128 * i, 128 * i + 128)
+        column = jnp.transpose(jnp.broadcast_to(root[:, rows], (128, 128)))
+        for h in range(4):
+            cols = slice(128 * h, 128 * h + 128)
+            weighted[rows, cols] = (features[rows, cols].astype(jnp.float32) * column).astype(jnp.bfloat16)
+    for o in range(1, 4):
+        ship(weighted.at[pl.ds(pl.multiple_of(((z + o) % 4) * 512, 512), 512), :], blocks.at[o], to_z(o))
+    kept = pltpu.make_async_copy(weighted.at[pl.ds(pl.multiple_of(z * 512, 512), 512), :], blocks.at[0], lsem.at[2])
+    kept.start()
+    redistributed = started[-3:]
+
     def mixed(row):
         rows = pl.ds(pl.multiple_of(row, 256), 256)
-        fine_rows = fine[rows, :]
-        pattern = jnp.concatenate([fine_rows * jnp.broadcast_to(coarse[rows, h : h + 1], (256, 128)) for h in range(16)], axis=1)
-        return jnp.dot(pattern, signed[...], preferred_element_type=jnp.float32)
+        return jnp.dot(pattern[rows, :], weighted[...], preferred_element_type=jnp.float32)
 
     halves = []
     for q in range(4):
         send[q] = mixed((1 - c) * 1024 + 256 * q)
-        if q == 0:
-            pl.semaphore_wait(barrier, 10)
         halves.append(ship(send.at[q], arrive.at[q], other))
+    slope = row_times(probability - labels[...].astype(jnp.float32), features[...], NN)
+    wide[...] = jnp.zeros((1, D), jnp.float32)
+    wide[:, pl.ds(pl.multiple_of(z * 512, 512), 512)] = slope * (1.0 / total_rows) + weights[...] * (REG / D / 32)
+    abuf[within] = wide[...]
+    near_copies = spread(abuf, within, 8, near)
     for q in range(4):
         keep[q] = mixed(c * 1024 + 256 * q)
     for q in range(4):
@@ -428,6 +482,8 @@
     for o in range(1, 4):
         first.append(ship(narrow.at[0, (x + o) % 4], xin.at[o - 1], to_x(o)))
         first.append(ship(narrow.at[1, (y + o) % 4], yin.at[o - 1], to_y(o)))
+    bbuf[y * 4 + z] = gathered(near_copies, abuf, 8)
+    far_copies = spread(bbuf, y * 4 + z, 16, far)
     for copy in first:
         copy.wait_recv()
     left_total = keep[x, :, :256]
@@ -512,20 +568,24 @@
             across.append(ship(ref, ref, other))
     for copy in across:
         copy.wait_recv()
+    residual[...] = -gathered(far_copies, bbuf, 16)
+    for copy in redistributed:
+        copy.wait_recv()
+    kept.wait()
     for copy in started:
         copy.wait_send()
 
 
-def sketch_rows(scale, signed, coarse, fine):
+def sketch_rows(scale, total_rows, features, weights, labels, signs, coarse, fine):
     vm = pl.BlockSpec(memory_space=pltpu.VMEM)
     anywhere = pl.BlockSpec(memory_space=pl.ANY)
     f32, bf16 = jnp.float32, jnp.bfloat16
     half = jax.ShapeDtypeStruct((2, 4, 4, 64, D // 2), bf16)
-    left, right = pl.pallas_call(
-        lambda *refs: sketch_kernel(scale, *refs),
-        out_shape=(half, half),
-        in_specs=[vm] * 3,
-        out_specs=(anywhere, anywhere),
+    left, right, residual, blocks = pl.pallas_call(
+        lambda *refs: sketch_kernel(scale, total_rows, *refs),
+        out_shape=(half, half, jax.ShapeDtypeStruct((1, D), f32), jax.ShapeDtypeStruct((4, 512, 512), bf16)),
+        in_specs=[vm] * 6,
+        out_specs=(anywhere, anywhere, vm, anywhere),
         scratch_shapes=[
             pltpu.VMEM((4, 256, 512), f32),
             pltpu.VMEM((4, 256, 512), f32),
@@ -537,14 +597,20 @@
             pltpu.VMEM((3, 64, 256), f32),
             pltpu.VMEM((3, 64, 256), f32),
             pltpu.VMEM((2, 64, 256), bf16),
-            pltpu.SemaphoreType.DMA((72,)),
-            pltpu.SemaphoreType.DMA((72,)),
-            pltpu.SemaphoreType.DMA((2,)),
+            pltpu.VMEM((D, 2048), bf16),
+            pltpu.VMEM((2048, 512), bf16),
+            pltpu.VMEM((1, D), f32),
+            pltpu.VMEM((4, 1, 2048), f32),
+            pltpu.VMEM((8, 1, D), f32),
+            pltpu.VMEM((16, 1, D), f32),
+            pltpu.SemaphoreType.DMA((112,)),
+            pltpu.SemaphoreType.DMA((112,)),
+            pltpu.SemaphoreType.DMA((3,)),
         ],
-        compiler_params=pltpu.CompilerParams(vmem_limit_bytes=32 * 2**20, collective_id=1, has_side_effects=True),
+        compiler_params=pltpu.CompilerParams(vmem_limit_bytes=36 * 2**20, collective_id=1, has_side_effects=True),
         name="sketch",
-    )(signed, coarse, fine)
-    return left.reshape(D, D // 2), right.reshape(D, D // 2)
+    )(features, weights, labels, signs, coarse, fine)
+    return left.reshape(D, D // 2), right.reshape(D, D // 2), residual, blocks
 
 
 def parity(common):
@@ -559,27 +625,22 @@
     ex_index = lax.axis_index("ex")
     total_rows = row_count * ex_count
     sample_count = samples.shape[0]
-    dense = features.astype(jnp.float32)
-    margins = lax.psum(jnp.dot(dense, weights, precision=HI), "feat")
-    probability = 1.0 / (1.0 + jnp.exp(-margins))
-    curvature = probability * (1.0 - probability)
-    grad_part = jnp.dot(probability - labels.astype(jnp.float32), dense, precision=HI)
-    weighted = (jnp.sqrt(curvature)[:, None] * dense).astype(jnp.bfloat16)
-    signed = weighted * signs.astype(jnp.bfloat16)[:, None]
     low, high = samples % row_count, samples // row_count
     coarse = parity((low[:, None] // 128) & lax.iota(jnp.int32, row_count // 128)[None, :])
     coarse = coarse * parity(high & ex_index)[:, None]
     fine = parity((low[:, None] % 128) & lax.iota(jnp.int32, 128)[None, :])
     scale = 1.0 / math.sqrt(total_rows * sample_count)
-    left, right = sketch_rows(scale, signed, coarse.astype(jnp.bfloat16), fine.astype(jnp.bfloat16))
-    factors = factor(left, right)
-    feat_index = lax.axis_index("feat")
-    part = row_count // 4
-    blocks = []
-    for o in range(4):
-        rows = lax.dynamic_slice_in_dim(weighted, ((feat_index + o) % 4) * part, part, 0)
-        blocks.append(lax.ppermute(rows, "feat", [(i, (i + o) % 4) for i in range(4)]) if o else rows)
-    out = pcg(total_rows, blocks, grad_part[None, :], factors, weights[None, :], radius[None, :])
+    left, right, residual, blocks = sketch_rows(
+        scale,
+        total_rows,
+        features,
+        weights[None, :],
+        labels[None, :],
+        signs[None, :],
+        coarse.astype(jnp.bfloat16),
+        fine.astype(jnp.bfloat16),
+    )
+    out = pcg(total_rows, blocks, residual, factor(left, right), weights[None, :], radius[None, :])
     return out[0]
 
 

time: 274 us -> 242 us (0.88)
  blocking collectives: 10.7 us -> 0 us
  local copies, waits for them, and re-layouts: 11 us -> 4.25 us
  matrix products: 4.22 us -> 0 us
  Pallas kernels: 238 us -> 234 us
  other arithmetic: 5.85 us -> 2.76 us
    pallas_call x1, Pallas kernels: 60.6 us -> 74.2 us  [sketch_rows(): pl.pallas_call(lambda *refs: sketch_kernel(scale, total_rows, *refs), out...]
    pallas_call x1, Pallas kernels: 78.1 us -> 66.9 us  [pcg(): pl.pallas_call(lambda *refs: pcg_kernel(total_rows, *refs), out_shape=jax...]
    psum x1 -> x0, blocking collectives: 10.7 us -> none  [local(): margins = lax.psum(jnp.dot(dense, weights, precision=HI), 'feat')]
    pallas_call x1, Pallas kernels: 99.3 us -> 93.5 us  [factor(): pl.pallas_call(factor_kernel, out_shape=(ups, ups, inverses, inverses), i...]
    dot_general x2 -> x0, matrix products: 4.22 us -> none  [the longest x1 3.31 us: local(): margins = lax.psum(jnp.dot(dense, weights, precision=HI), 'feat')]
    unnamed x19 -> x11, local copies, waits for them, and re-layouts: 8.28 us -> 4.25 us
    mul x1 -> x0, other arithmetic: 3.06 us -> none  [local(): signed = weighted * signs.astype(jnp.bfloat16)[:, None]]
  transfers between devices with their start and end apart: 3 -> 0, of which waited for: 0 -> 0; matrix products, arithmetic and copies ran while one was open for 1% -> 0% of each run, Pallas kernels for 58% -> 0%
where the time goes in v4:
time: 242 us
  Pallas kernels  234 us (97%)
  local copies, waits for them, and re-layouts  4.25 us (2%)
  other arithmetic  2.76 us (1%)
    pallas_call x1, Pallas kernels, factor(): pl.pallas_call(factor_kernel, out_shape=(ups, ups, inverses, inverses), i...  93.5 us
    pallas_call x1, Pallas kernels, sketch_rows(): pl.pallas_call(lambda *refs: sketch_kernel(scale, total_rows, *refs), out...  74.2 us
    pallas_call x1, Pallas kernels, pcg(): pl.pallas_call(lambda *refs: pcg_kernel(total_rows, *refs), out_shape=jax...  66.9 us

profile of v4, /device:TPU:1, one launch (start us, length us, event | category | flops | bytes accessed | tf_op | source)
XLA Modules:
  0.0 242.2 jit_solution(18384429670623753519)
XLA Ops:
  0.0 0.7 add_select_fusion
  0.7 1.4 fusion.4.refs_4_
  2.1 0.7 fusion.8.refs_5_
  2.8 0.0 copy-start
  2.8 1.6 copy-done
  4.4 0.0 copy-start.1
  4.4 0.7 copy-done.1
  5.1 0.0 copy-start.2
  5.1 0.7 copy-done.2
  5.8 0.0 copy-start.3
  5.8 0.7 copy-done.3
  6.4 74.2 %sketch.1 = (bf16[2,4,4,64,1024]{4,3,2,1,0:T(8,128)(2,1)S(1)}, bf16[2,4,4,64,1024]{4,3,2,1,0:T(8,128)(2,1)S(1)}, f32[1,2048]{1,0:T(1,128)S(1)}, bf16[4,512,512]{2,1,0:T(8,128)(2,1)S(1)}) custom-call(bf16[2048,512]{1,0:T(8,128)(2,1)S(1)} %copy-done, f32[1,512]{1,0:T(1,128)S(1)} %bitcast.11, s32[1,2048]{1,0:T(1,128)S(1)} %bitcast.8, s32[1,2048]{1,0:T(1,128)S(1)} %bitcast.9, ...), custom_call_target="tpu_custom_call" | custom-call | tf_op jit(solution)/shard_map/sketch/pallas_call | solution.py:584
  80.6 0.0 copy-start.4
  80.6 93.5 %factor.1 = (bf16[6,512,512]{2,1,0:T(8,128)(2,1)S(1)}, bf16[6,512,512]{2,1,0:T(8,128)(2,1)S(1)}, bf16[4,512,512]{2,1,0:T(8,128)(2,1)S(1)}, bf16[4,512,512]{2,1,0:T(8,128)(2,1)S(1)}) custom-call(bf16[2048,1024]{1,0:T(8,128)(2,1)S(1)} %bitcast.13, bf16[2048,1024]{1,0:T(8,128)(2,1)S(1)} %bitcast.14), custom_call_target="tpu_custom_call" | custom-call | flops 60000002048 | bytes 18874368 | tf_op jit(solution)/shard_map/factor/pallas_call | solution.py:212
  174.7 0.0 copy-done.4
  174.8 66.9 %pcg.1 = f32[1,512]{1,0:T(1,128)S(1)} custom-call(bf16[4,512,512]{2,1,0:T(8,128)(2,1)S(1)} %get-tuple-element.13.refs_0_, f32[1,2048]{1,0:T(1,128)S(1)} %get-tuple-element.14.refs_1_, bf16[6,512,512]{2,1,0:T(8,128)(2,1)S(1)} %get-tuple-element.17.refs_2_, bf16[6,512,512]{2,1,0:T(8,128)(2,1)S(1)} %get-tuple-element.18.refs_3_, ...), custom_call_target="tpu_custom_call" | custom-call | tf_op jit(solution)/shard_map/pcg/pallas_call | solution.py:352
  241.6 0.6 copy.12
Async XLA Ops:
  2.8 1.6 copy-start
  4.4 0.7 copy-start.1
  5.1 0.7 copy-start.2
  5.8 0.7 copy-start.3
  80.6 94.1 %copy-start.4 = (f32[512]{0:T(512)S(1)}, f32[512]{0:T(512)}, u32[]{:S(2)}) copy-start(f32[512]{0:T(512)} %param.7) | copy-start | bytes 6148

commit v5 on v4

--- a/solution.py
+++ b/solution.py
@@ -19,6 +19,15 @@
 def split2(value):
     high = value.astype(jnp.bfloat16)
     return high, (value - high.astype(jnp.float32)).astype(jnp.bfloat16)
+
+
+def dot3(left, right, dims):
+    (lc,), (rc,) = dims[0]
+    lh, ll = split2(left)
+    rh, rl = split2(right)
+    left = jnp.concatenate([lh, lh, ll], axis=lc)
+    right = jnp.concatenate([rh, rl, rh], axis=rc)
+    return lax.dot_general(left, right, dims, preferred_element_type=jnp.float32)
 
 
 def block_inverse(block):
@@ -124,8 +133,8 @@
                         gram[512 * a + 256 : 512 * a + 512, 512 * a : 512 * a + 256] = jnp.zeros((256, 256), jnp.float32)
 
     def join(top, bottom, cross):
-        middle = lax.dot_general(cross, top, TN, precision=HI, preferred_element_type=jnp.float32)
-        edge = -lax.dot_general(bottom, middle, NN, precision=HI, preferred_element_type=jnp.float32)
+        middle = dot3(cross, top, TN)
+        edge = -dot3(bottom, middle, NN)
         zero = jnp.zeros_like(top)
         return jnp.concatenate([jnp.concatenate([top, zero], axis=1), jnp.concatenate([edge, bottom], axis=1)], axis=0)
 
@@ -141,9 +150,9 @@
             corner[2 + h] = block_inverse(corner[h])
 
             if h == 0:
-                cross = lax.dot_general(corner[2], gram[upper, lower], NN, precision=HI, preferred_element_type=jnp.float32)
+                cross = dot3(corner[2], gram[upper, lower], NN)
                 corner[4] = cross
-                corner[1] = gram[lower, lower] - lax.dot_general(cross, cross, TN, precision=HI, preferred_element_type=jnp.float32)
+                corner[1] = gram[lower, lower] - dot3(cross, cross, TN)
 
             return carry
 
@@ -375,7 +384,7 @@
 def sketch_kernel(
     scale, total_rows, features, weights, labels, signs, coarse, fine,
     left, right, residual, blocks,
-    send, keep, arrive, narrow, xin, yin, stage, xlast, ylast, mine, pattern, weighted, wide, zbuf, abuf, bbuf, ssem, rsem, lsem,
+    send, arrive, narrow, xin, yin, stage, xlast, ylast, mine, pattern, weighted, wide, zbuf, abuf, bbuf, ssem, rsem, lsem,
 ):
     ex = lax.axis_index("ex")
     z = lax.axis_index("feat")
@@ -457,37 +466,37 @@
     kept.start()
     redistributed = started[-3:]
 
-    def mixed(row):
-        rows = pl.ds(pl.multiple_of(row, 256), 256)
-        return jnp.dot(pattern[rows, :], weighted[...], preferred_element_type=jnp.float32)
+    def mixed(half, o):
+        parts = []
+        for block, cols in (((x + o) % 4, slice(0, 256)), ((y + o) % 4, slice(256, 512))):
+            rows = pl.ds(pl.multiple_of(half * 1024 + block * 256, 256), 256)
+            parts.append(jnp.dot(pattern[rows, :], weighted[:, cols], preferred_element_type=jnp.float32))
+        return parts
 
     halves = []
-    for q in range(4):
-        send[q] = mixed((1 - c) * 1024 + 256 * q)
-        halves.append(ship(send.at[q], arrive.at[q], other))
+    for at, o in enumerate((1, 2, 3, 0)):
+        send[at, 0], send[at, 1] = mixed(1 - c, o)
+        halves.append(ship(send.at[at], arrive.at[at], other))
     slope = row_times(probability - labels[...].astype(jnp.float32), features[...], NN)
     wide[...] = jnp.zeros((1, D), jnp.float32)
     wide[:, pl.ds(pl.multiple_of(z * 512, 512), 512)] = slope * (1.0 / total_rows) + weights[...] * (REG / D / 32)
     abuf[within] = wide[...]
     near_copies = spread(abuf, within, 8, near)
-    for q in range(4):
-        keep[q] = mixed(c * 1024 + 256 * q)
-    for q in range(4):
-        halves[q].wait_recv()
-        total = keep[q] + arrive[q]
-        keep[q] = total
-        narrow[0, q] = total[:, :256].astype(jnp.bfloat16)
-        narrow[1, q] = total[:, 256:].astype(jnp.bfloat16)
     first = []
-    for o in range(1, 4):
-        first.append(ship(narrow.at[0, (x + o) % 4], xin.at[o - 1], to_x(o)))
-        first.append(ship(narrow.at[1, (y + o) % 4], yin.at[o - 1], to_y(o)))
+    for at, o in enumerate((1, 2, 3, 0)):
+        left_total, right_total = mixed(c, o)
+        halves[at].wait_recv()
+        left_total = left_total + arrive[at, 0]
+        right_total = right_total + arrive[at, 1]
+        if o > 0:
+            narrow[0, at] = left_total.astype(jnp.bfloat16)
+            narrow[1, at] = right_total.astype(jnp.bfloat16)
+            first.append(ship(narrow.at[0, at], xin.at[at], to_x(o)))
+            first.append(ship(narrow.at[1, at], yin.at[at], to_y(o)))
     bbuf[y * 4 + z] = gathered(near_copies, abuf, 8)
     far_copies = spread(bbuf, y * 4 + z, 16, far)
     for copy in first:
         copy.wait_recv()
-    left_total = keep[x, :, :256]
-    right_total = keep[y, :, 256:]
     for o in range(3):
         left_total = left_total + xin[o].astype(jnp.float32)
         right_total = right_total + yin[o].astype(jnp.float32)
@@ -521,7 +530,6 @@
     def same(ref, peer):
         return (ref, ref, peer)
 
-    here_left, here_right = left.at[c, x, y], right.at[c, y, x]
     copies = pass_on(
         [
             (mine.at[0, big], left.at[c, x, y, big, cols], to_z),
@@ -544,28 +552,44 @@
     )
     for copy in copies:
         copy.wait_recv()
-    copies = pass_on(
-        [
-            same(left.at[c, x, every, big, :], to_x),
-            same(right.at[c, y, every, big, :], to_y),
-            same(left.at[c, every, every, small, cols], to_z),
-            same(right.at[c, every, every, small, cols], to_z),
-        ]
-    )
     across = []
-    for o in range(4):
-        if o > 0:
-            for copy in copies[4 * o - 4 : 4 * o]:
-                copy.wait_recv()
-        from_x, from_y = (x + 4 - o) % 4, (y + 4 - o) % 4
-        from_z = pl.ds(pl.multiple_of(((z + 4 - o) % 4) * 256, 256), 256)
-        for ref in (
-            left.at[c, from_x, every, big, :],
-            right.at[c, from_y, every, big, :],
-            left.at[c, every, every, small, from_z],
-            right.at[c, every, every, small, from_z],
-        ):
-            across.append(ship(ref, ref, other))
+
+    def cross(ref):
+        across.append(ship(ref, ref, other))
+
+    def zcols(o):
+        return pl.ds(pl.multiple_of(((z + o) % 4) * 256, 256), 256)
+
+    def x_piece(o, part):
+        return left.at[c, (x + o) % 4, pl.ds(2 * part, 2), big, :]
+
+    def y_piece(o, part):
+        return right.at[c, (y + o) % 4, pl.ds(2 * part, 2), big, :]
+
+    def z_piece(o, part):
+        return (left, right)[part].at[c, every, every, small, zcols(o)]
+
+    streams = ((x_piece, to_x), (y_piece, to_y), (z_piece, to_z))
+    up, down, late = [], [], []
+    for piece, peer in streams:
+        up.append(ship(piece(0, 0), piece(0, 0), peer(1)))
+        down.append(ship(piece(0, 1), piece(0, 1), peer(3)))
+    for piece, peer in streams:
+        late.append((ship(piece(0, 1), piece(0, 1), peer(1)), piece(3, 1)))
+        late.append((ship(piece(0, 0), piece(0, 0), peer(3)), piece(1, 0)))
+    for piece, peer in streams:
+        cross(piece(0, 0))
+        cross(piece(0, 1))
+    for at, (piece, peer) in enumerate(streams):
+        up[at].wait_recv()
+        late.append((ship(piece(3, 0), piece(3, 0), peer(1)), piece(2, 0)))
+        cross(piece(3, 0))
+        down[at].wait_recv()
+        late.append((ship(piece(1, 1), piece(1, 1), peer(3)), piece(2, 1)))
+        cross(piece(1, 1))
+    for copy, ref in late:
+        copy.wait_recv()
+        cross(ref)
     for copy in across:
         copy.wait_recv()
     residual[...] = -gathered(far_copies, bbuf, 16)
@@ -587,10 +611,9 @@
         in_specs=[vm] * 6,
         out_specs=(anywhere, anywhere, vm, anywhere),
         scratch_shapes=[
-            pltpu.VMEM((4, 256, 512), f32),
-            pltpu.VMEM((4, 256, 512), f32),
-            pltpu.VMEM((4, 256, 512), f32),
-            pltpu.VMEM((2, 4, 256, 256), bf16),
+            pltpu.VMEM((4, 2, 256, 256), f32),
+            pltpu.VMEM((4, 2, 256, 256), f32),
+            pltpu.VMEM((2, 3, 256, 256), bf16),
             pltpu.VMEM((3, 256, 256), bf16),
             pltpu.VMEM((3, 256, 256), bf16),
             pltpu.VMEM((2, 4, 64, 256), f32),
@@ -603,8 +626,8 @@
             pltpu.VMEM((4, 1, 2048), f32),
             pltpu.VMEM((8, 1, D), f32),
             pltpu.VMEM((16, 1, D), f32),
-            pltpu.SemaphoreType.DMA((112,)),
-            pltpu.SemaphoreType.DMA((112,)),
+            pltpu.SemaphoreType.DMA((120,)),
+            pltpu.SemaphoreType.DMA((120,)),
             pltpu.SemaphoreType.DMA((3,)),
         ],
         compiler_params=pltpu.CompilerParams(vmem_limit_bytes=36 * 2**20, collective_id=1, has_side_effects=True),

time: 242 us -> 232 us (0.959)
  Pallas kernels: 234 us -> 224 us
    pallas_call x1, Pallas kernels: 74.2 us -> 68.3 us  [sketch_rows(): pl.pallas_call(lambda *refs: sketch_kernel(scale, total_rows, *refs), out...]
    pallas_call x1, Pallas kernels: 93.5 us -> 89.7 us  [factor(): pl.pallas_call(factor_kernel, out_shape=(ups, ups, inverses, inverses), i...]
where the time goes in v5:
time: 232 us
  Pallas kernels  224 us (97%)
  local copies, waits for them, and re-layouts  4.25 us (2%)
  other arithmetic  2.76 us (1%)
    pallas_call x1, Pallas kernels, factor(): pl.pallas_call(factor_kernel, out_shape=(ups, ups, inverses, inverses), i...  89.7 us
    pallas_call x1, Pallas kernels, sketch_rows(): pl.pallas_call(lambda *refs: sketch_kernel(scale, total_rows, *refs), out...  68.3 us
    pallas_call x1, Pallas kernels, pcg(): pl.pallas_call(lambda *refs: pcg_kernel(total_rows, *refs), out_shape=jax...  65.8 us

profile of v5, /device:TPU:1, one launch (start us, length us, event | category | flops | bytes accessed | tf_op | source)
XLA Modules:
  0.0 231.6 jit_solution(15033691051270535438)
XLA Ops:
  0.0 0.7 add_select_fusion
  0.7 1.4 fusion.4.refs_4_
  2.1 0.7 fusion.8.refs_5_
  2.8 0.0 copy-start
  2.8 1.6 copy-done
  4.4 0.0 copy-start.1
  4.4 0.7 copy-done.1
  5.1 0.0 copy-start.2
  5.1 0.7 copy-done.2
  5.8 0.0 copy-start.3
  5.8 0.7 copy-done.3
  6.4 68.3 %sketch.1 = (bf16[2,4,4,64,1024]{4,3,2,1,0:T(8,128)(2,1)S(1)}, bf16[2,4,4,64,1024]{4,3,2,1,0:T(8,128)(2,1)S(1)}, f32[1,2048]{1,0:T(1,128)S(1)}, bf16[4,512,512]{2,1,0:T(8,128)(2,1)S(1)}) custom-call(bf16[2048,512]{1,0:T(8,128)(2,1)S(1)} %copy-done, f32[1,512]{1,0:T(1,128)S(1)} %bitcast.11, s32[1,2048]{1,0:T(1,128)S(1)} %bitcast.8, s32[1,2048]{1,0:T(1,128)S(1)} %bitcast.9, ...), custom_call_target="tpu_custom_call" | custom-call | tf_op jit(solution)/shard_map/sketch/pallas_call | solution.py:608
  74.8 0.0 copy-start.4
  74.8 89.7 %factor.1 = (bf16[6,512,512]{2,1,0:T(8,128)(2,1)S(1)}, bf16[6,512,512]{2,1,0:T(8,128)(2,1)S(1)}, bf16[4,512,512]{2,1,0:T(8,128)(2,1)S(1)}, bf16[4,512,512]{2,1,0:T(8,128)(2,1)S(1)}) custom-call(bf16[2048,1024]{1,0:T(8,128)(2,1)S(1)} %bitcast.13, bf16[2048,1024]{1,0:T(8,128)(2,1)S(1)} %bitcast.14), custom_call_target="tpu_custom_call" | custom-call | flops 60000002048 | bytes 18874368 | tf_op jit(solution)/shard_map/factor/pallas_call | solution.py:221
  165.2 0.0 copy-done.4
  165.2 65.8 %pcg.1 = f32[1,512]{1,0:T(1,128)S(1)} custom-call(bf16[4,512,512]{2,1,0:T(8,128)(2,1)S(1)} %get-tuple-element.13.refs_0_, f32[1,2048]{1,0:T(1,128)S(1)} %get-tuple-element.14.refs_1_, bf16[6,512,512]{2,1,0:T(8,128)(2,1)S(1)} %get-tuple-element.17.refs_2_, bf16[6,512,512]{2,1,0:T(8,128)(2,1)S(1)} %get-tuple-element.18.refs_3_, ...), custom_call_target="tpu_custom_call" | custom-call | tf_op jit(solution)/shard_map/pcg/pallas_call | solution.py:361
  231.0 0.6 copy.12
Async XLA Ops:
  2.8 1.6 copy-start
  4.4 0.7 copy-start.1
  5.1 0.7 copy-start.2
  5.8 0.7 copy-start.3
  74.8 90.4 %copy-start.4 = (f32[512]{0:T(512)S(1)}, f32[512]{0:T(512)}, u32[]{:S(2)}) copy-start(f32[512]{0:T(512)} %param.7) | copy-start | bytes 6148

commit v6 on v5

--- a/solution.py
+++ b/solution.py
@@ -278,7 +278,6 @@
         pl.semaphore_signal(barrier, inc=1, device_id=near(o), device_id_type=MESH)
     for o in range(1, 16):
         pl.semaphore_signal(barrier, inc=1, device_id=far(o), device_id_type=MESH)
-    pl.semaphore_wait(barrier, 22)
 
     def exchange(value, buf, turn, me, count, peer, send, recv):
         buf[turn, me] = value
@@ -344,6 +343,11 @@
         for o in range(4):
             part = lax.dot_general(stacked, blocks[o], NN, preferred_element_type=jnp.float32)
             wide[:, columns(o)] = jnp.sum(part, axis=0, keepdims=True)
+
+        @pl.when(number == 0)
+        def _():
+            pl.semaphore_wait(barrier, 22)
+
         curved = everywhere(wide[...], number) * (1.0 / total_rows) + ridge * direction
         step_size = inner_now / dot(direction, curved)
         return answer + step_size * direction, residual - step_size * curved, direction, inner_now
@@ -384,7 +388,7 @@
 def sketch_kernel(
     scale, total_rows, features, weights, labels, signs, coarse, fine,
     left, right, residual, blocks,
-    send, arrive, narrow, xin, yin, stage, xlast, ylast, mine, pattern, weighted, wide, zbuf, abuf, bbuf, ssem, rsem, lsem,
+    send, arrive, narrow, xin, yin, stage, xlast, ylast, mine, pattern, weighted, relay, wide, zbuf, abuf, bbuf, ssem, rsem, lsem,
 ):
     ex = lax.axis_index("ex")
     z = lax.axis_index("feat")
@@ -460,11 +464,14 @@
         for h in range(4):
             cols = slice(128 * h, 128 * h + 128)
             weighted[rows, cols] = (features[rows, cols].astype(jnp.float32) * column).astype(jnp.bfloat16)
-    for o in range(1, 4):
-        ship(weighted.at[pl.ds(pl.multiple_of(((z + o) % 4) * 512, 512), 512), :], blocks.at[o], to_z(o))
+
+    def rows_for(o, part, size):
+        return weighted.at[pl.ds(pl.multiple_of(((z + o) % 4) * 512 + part * 256, 256), size), :]
+
+    passing = [ship(rows_for(2, 0, 256), relay.at[0], to_z(1)), ship(rows_for(2, 1, 256), relay.at[1], to_z(3))]
+    redistributed = [ship(rows_for(1, 0, 512), blocks.at[1], to_z(1)), ship(rows_for(3, 0, 512), blocks.at[3], to_z(3))]
     kept = pltpu.make_async_copy(weighted.at[pl.ds(pl.multiple_of(z * 512, 512), 512), :], blocks.at[0], lsem.at[2])
     kept.start()
-    redistributed = started[-3:]
 
     def mixed(half, o):
         parts = []
@@ -493,6 +500,9 @@
             narrow[1, at] = right_total.astype(jnp.bfloat16)
             first.append(ship(narrow.at[0, at], xin.at[at], to_x(o)))
             first.append(ship(narrow.at[1, at], yin.at[at], to_y(o)))
+    for part, o in ((0, 1), (1, 3)):
+        passing[part].wait_recv()
+        redistributed.append(ship(relay.at[part], blocks.at[2, pl.ds(256 * part, 256)], to_z(o)))
     bbuf[y * 4 + z] = gathered(near_copies, abuf, 8)
     far_copies = spread(bbuf, y * 4 + z, 16, far)
     for copy in first:
@@ -622,6 +632,7 @@
             pltpu.VMEM((2, 64, 256), bf16),
             pltpu.VMEM((D, 2048), bf16),
             pltpu.VMEM((2048, 512), bf16),
+            pltpu.VMEM((2, 256, 512), bf16),
             pltpu.VMEM((1, D), f32),
             pltpu.VMEM((4, 1, 2048), f32),
             pltpu.VMEM((8, 1, D), f32),

time: 232 us -> 228 us (0.983)
  Pallas kernels: 224 us -> 220 us
where the time goes in v6:
time: 228 us
  Pallas kernels  220 us (96%)
  local copies, waits for them, and re-layouts  4.25 us (2%)
  other arithmetic  2.76 us (1%)
    pallas_call x1, Pallas kernels, factor(): pl.pallas_call(factor_kernel, out_shape=(ups, ups, inverses, inverses), i...  89.7 us
    pallas_call x1, Pallas kernels, sketch_rows(): pl.pallas_call(lambda *refs: sketch_kernel(scale, total_rows, *refs), out...  67 us
    pallas_call x1, Pallas kernels, pcg(): pl.pallas_call(lambda *refs: pcg_kernel(total_rows, *refs), out_shape=jax...  63.8 us

profile of v6, /device:TPU:1, one launch (start us, length us, event | category | flops | bytes accessed | tf_op | source)
XLA Modules:
  0.0 228.2 jit_solution(15292292326675781839)
XLA Ops:
  0.0 0.7 add_select_fusion
  0.7 1.4 fusion.4.refs_4_
  2.1 0.7 fusion.8.refs_5_
  2.8 0.0 copy-start
  2.8 1.6 copy-done
  4.4 0.0 copy-start.1
  4.4 0.7 copy-done.1
  5.1 0.0 copy-start.2
  5.1 0.7 copy-done.2
  5.8 0.0 copy-start.3
  5.8 0.7 copy-done.3
  6.4 67.0 %sketch.1 = (bf16[2,4,4,64,1024]{4,3,2,1,0:T(8,128)(2,1)S(1)}, bf16[2,4,4,64,1024]{4,3,2,1,0:T(8,128)(2,1)S(1)}, f32[1,2048]{1,0:T(1,128)S(1)}, bf16[4,512,512]{2,1,0:T(8,128)(2,1)S(1)}) custom-call(bf16[2048,512]{1,0:T(8,128)(2,1)S(1)} %copy-done, f32[1,512]{1,0:T(1,128)S(1)} %bitcast.11, s32[1,2048]{1,0:T(1,128)S(1)} %bitcast.8, s32[1,2048]{1,0:T(1,128)S(1)} %bitcast.9, ...), custom_call_target="tpu_custom_call" | custom-call | tf_op jit(solution)/shard_map/sketch/pallas_call | solution.py:618
  73.4 0.0 copy-start.4
  73.4 89.7 %factor.1 = (bf16[6,512,512]{2,1,0:T(8,128)(2,1)S(1)}, bf16[6,512,512]{2,1,0:T(8,128)(2,1)S(1)}, bf16[4,512,512]{2,1,0:T(8,128)(2,1)S(1)}, bf16[4,512,512]{2,1,0:T(8,128)(2,1)S(1)}) custom-call(bf16[2048,1024]{1,0:T(8,128)(2,1)S(1)} %bitcast.13, bf16[2048,1024]{1,0:T(8,128)(2,1)S(1)} %bitcast.14), custom_call_target="tpu_custom_call" | custom-call | flops 60000002048 | bytes 18874368 | tf_op jit(solution)/shard_map/factor/pallas_call | solution.py:221
  163.8 0.0 copy-done.4
  163.8 63.8 %pcg.1 = f32[1,512]{1,0:T(1,128)S(1)} custom-call(bf16[4,512,512]{2,1,0:T(8,128)(2,1)S(1)} %get-tuple-element.13.refs_0_, f32[1,2048]{1,0:T(1,128)S(1)} %get-tuple-element.14.refs_1_, bf16[6,512,512]{2,1,0:T(8,128)(2,1)S(1)} %get-tuple-element.17.refs_2_, bf16[6,512,512]{2,1,0:T(8,128)(2,1)S(1)} %get-tuple-element.18.refs_3_, ...), custom_call_target="tpu_custom_call" | custom-call | tf_op jit(solution)/shard_map/pcg/pallas_call | solution.py:365
  227.6 0.6 copy.12
Async XLA Ops:
  2.8 1.6 copy-start
  4.4 0.7 copy-start.1
  5.1 0.7 copy-start.2
  5.8 0.7 copy-start.3
  73.4 90.4 %copy-start.4 = (f32[512]{0:T(512)S(1)}, f32[512]{0:T(512)}, u32[]{:S(2)}) copy-start(f32[512]{0:T(512)} %param.7) | copy-start | bytes 6148

commit v7 on v6

--- a/solution.py
+++ b/solution.py
@@ -386,10 +386,18 @@
     return jnp.sum(lax.dot_general(pieces(row), matrix, dims, preferred_element_type=jnp.float32), axis=0, keepdims=True)
 
 def sketch_kernel(
-    scale, total_rows, features, weights, labels, signs, coarse, fine,
+    scale, total_rows, all_features, all_weights, all_labels, all_signs, coarse, fine,
     left, right, residual, blocks,
-    send, arrive, narrow, xin, yin, stage, xlast, ylast, mine, pattern, weighted, relay, wide, zbuf, abuf, bbuf, ssem, rsem, lsem,
+    send, arrive, narrow, xin, yin, stage, xlast, ylast, mine, pattern, weighted, relay, wide, zbuf, abuf, bbuf, features, weights, labels, signs, ssem, rsem, lsem,
 ):
+    fetches = [
+        pltpu.make_async_copy(src, dst, lsem.at[3 + at])
+        for at, (src, dst) in enumerate(
+            ((all_features, features), (all_weights, weights), (all_labels, labels), (all_signs, signs))
+        )
+    ]
+    for fetch in fetches:
+        fetch.start()
     ex = lax.axis_index("ex")
     z = lax.axis_index("feat")
     y, x, c = ex // 8, (ex // 2) % 4, ex % 2
@@ -441,6 +449,8 @@
             totals = [totals[i] + totals[i + 1] for i in range(0, len(totals), 2)]
         return totals[0]
 
+    for fetch in fetches:
+        fetch.wait()
     zbuf[z] = row_times(weights[...], features[...], NT)
     pl.semaphore_wait(barrier, 22)
     margin_copies = spread(zbuf, z, 4, to_z)
@@ -618,7 +628,7 @@
     left, right, residual, blocks = pl.pallas_call(
         lambda *refs: sketch_kernel(scale, total_rows, *refs),
         out_shape=(half, half, jax.ShapeDtypeStruct((1, D), f32), jax.ShapeDtypeStruct((4, 512, 512), bf16)),
-        in_specs=[vm] * 6,
+        in_specs=[pl.BlockSpec(memory_space=pltpu.HBM)] * 4 + [vm] * 2,
         out_specs=(anywhere, anywhere, vm, anywhere),
         scratch_shapes=[
             pltpu.VMEM((4, 2, 256, 256), f32),
@@ -637,9 +647,13 @@
             pltpu.VMEM((4, 1, 2048), f32),
             pltpu.VMEM((8, 1, D), f32),
             pltpu.VMEM((16, 1, D), f32),
+            pltpu.VMEM((2048, 512), bf16),
+            pltpu.VMEM((1, 512), f32),
+            pltpu.VMEM((1, 2048), jnp.int32),
+            pltpu.VMEM((1, 2048), jnp.int32),
             pltpu.SemaphoreType.DMA((120,)),
             pltpu.SemaphoreType.DMA((120,)),
-            pltpu.SemaphoreType.DMA((3,)),
+            pltpu.SemaphoreType.DMA((7,)),
         ],
         compiler_params=pltpu.CompilerParams(vmem_limit_bytes=36 * 2**20, collective_id=1, has_side_effects=True),
         name="sketch",
@@ -659,10 +673,10 @@
     ex_index = lax.axis_index("ex")
     total_rows = row_count * ex_count
     sample_count = samples.shape[0]
-    low, high = samples % row_count, samples // row_count
-    coarse = parity((low[:, None] // 128) & lax.iota(jnp.int32, row_count // 128)[None, :])
+    low, high = samples & (row_count - 1), samples >> (row_count.bit_length() - 1)
+    coarse = parity((low[:, None] >> 7) & lax.iota(jnp.int32, row_count // 128)[None, :])
     coarse = coarse * parity(high & ex_index)[:, None]
-    fine = parity((low[:, None] % 128) & lax.iota(jnp.int32, 128)[None, :])
+    fine = parity((low[:, None] & 127) & lax.iota(jnp.int32, 128)[None, :])
     scale = 1.0 / math.sqrt(total_rows * sample_count)
     left, right, residual, blocks = sketch_rows(
         scale,

time: 228 us -> 229 us (level)
  no operation moved by 1% of the time
where the time goes in v7:
time: 229 us
  Pallas kernels  221 us (97%)
  local copies, waits for them, and re-layouts  4.25 us (2%)
  other arithmetic  2.75 us (1%)
    pallas_call x1, Pallas kernels, factor(): pl.pallas_call(factor_kernel, out_shape=(ups, ups, inverses, inverses), i...  89.7 us
    pallas_call x1, Pallas kernels, sketch_rows(): pl.pallas_call(lambda *refs: sketch_kernel(scale, total_rows, *refs), out...  67.4 us
    pallas_call x1, Pallas kernels, pcg(): pl.pallas_call(lambda *refs: pcg_kernel(total_rows, *refs), out_shape=jax...  63.8 us

profile of v7, /device:TPU:1, one launch (start us, length us, event | category | flops | bytes accessed | tf_op | source)
XLA Modules:
  0.0 228.7 jit_solution(14208514814938012011)
XLA Ops:
  0.0 0.7 and_and_fusion
  0.7 1.4 fusion.4.refs_4_
  2.1 0.7 fusion.8.refs_5_
  2.8 0.0 copy-start
  2.8 1.6 copy-done
  4.4 0.0 copy-start.1
  4.4 0.7 copy-done.1
  5.1 0.0 copy-start.2
  5.1 0.7 copy-done.2
  5.8 0.0 copy-start.3
  5.8 0.7 copy-done.3
  6.4 67.4 %sketch.1 = (bf16[2,4,4,64,1024]{4,3,2,1,0:T(8,128)(2,1)S(1)}, bf16[2,4,4,64,1024]{4,3,2,1,0:T(8,128)(2,1)S(1)}, f32[1,2048]{1,0:T(1,128)S(1)}, bf16[4,512,512]{2,1,0:T(8,128)(2,1)S(1)}) custom-call(bf16[2048,512]{1,0:T(8,128)(2,1)S(1)} %copy-done, f32[1,512]{1,0:T(1,128)S(1)} %bitcast.11, s32[1,2048]{1,0:T(1,128)S(1)} %bitcast.8, s32[1,2048]{1,0:T(1,128)S(1)} %bitcast.9, ...), custom_call_target="tpu_custom_call" | custom-call | tf_op jit(solution)/shard_map/sketch/pallas_call | solution.py:628
  73.9 0.0 copy-start.4
  73.9 89.7 %factor.1 = (bf16[6,512,512]{2,1,0:T(8,128)(2,1)S(1)}, bf16[6,512,512]{2,1,0:T(8,128)(2,1)S(1)}, bf16[4,512,512]{2,1,0:T(8,128)(2,1)S(1)}, bf16[4,512,512]{2,1,0:T(8,128)(2,1)S(1)}) custom-call(bf16[2048,1024]{1,0:T(8,128)(2,1)S(1)} %bitcast.13, bf16[2048,1024]{1,0:T(8,128)(2,1)S(1)} %bitcast.14), custom_call_target="tpu_custom_call" | custom-call | flops 60000002048 | bytes 18874368 | tf_op jit(solution)/shard_map/factor/pallas_call | solution.py:221
  164.3 0.0 copy-done.4
  164.3 63.8 %pcg.1 = f32[1,512]{1,0:T(1,128)S(1)} custom-call(bf16[4,512,512]{2,1,0:T(8,128)(2,1)S(1)} %get-tuple-element.13.refs_0_, f32[1,2048]{1,0:T(1,128)S(1)} %get-tuple-element.14.refs_1_, bf16[6,512,512]{2,1,0:T(8,128)(2,1)S(1)} %get-tuple-element.17.refs_2_, bf16[6,512,512]{2,1,0:T(8,128)(2,1)S(1)} %get-tuple-element.18.refs_3_, ...), custom_call_target="tpu_custom_call" | custom-call | tf_op jit(solution)/shard_map/pcg/pallas_call | solution.py:365
  228.1 0.6 copy.12
Async XLA Ops:
  2.8 1.6 copy-start
  4.4 0.7 copy-start.1
  5.1 0.7 copy-start.2
  5.8 0.7 copy-start.3
  73.9 90.4 %copy-start.4 = (f32[512]{0:T(512)S(1)}, f32[512]{0:T(512)}, u32[]{:S(2)}) copy-start(f32[512]{0:T(512)} %param.7) | copy-start | bytes 6148

commit v8 on v6

--- a/solution.py
+++ b/solution.py
@@ -388,7 +388,7 @@
 def sketch_kernel(
     scale, total_rows, features, weights, labels, signs, coarse, fine,
     left, right, residual, blocks,
-    send, arrive, narrow, xin, yin, stage, xlast, ylast, mine, pattern, weighted, relay, wide, zbuf, abuf, bbuf, ssem, rsem, lsem,
+    send, arrive, parcel, xin, yin, stage, xlast, ylast, mine, pattern, weighted, relay, wide, zbuf, abuf, bbuf, ssem, rsem, lsem,
 ):
     ex = lax.axis_index("ex")
     z = lax.axis_index("feat")
@@ -496,10 +496,10 @@
         left_total = left_total + arrive[at, 0]
         right_total = right_total + arrive[at, 1]
         if o > 0:
-            narrow[0, at] = left_total.astype(jnp.bfloat16)
-            narrow[1, at] = right_total.astype(jnp.bfloat16)
-            first.append(ship(narrow.at[0, at], xin.at[at], to_x(o)))
-            first.append(ship(narrow.at[1, at], yin.at[at], to_y(o)))
+            parcel[0, at] = left_total
+            parcel[1, at] = right_total
+            first.append(ship(parcel.at[0, at], xin.at[at], to_x(o)))
+            first.append(ship(parcel.at[1, at], yin.at[at], to_y(o)))
     for part, o in ((0, 1), (1, 3)):
         passing[part].wait_recv()
         redistributed.append(ship(relay.at[part], blocks.at[2, pl.ds(256 * part, 256)], to_z(o)))
@@ -508,8 +508,8 @@
     for copy in first:
         copy.wait_recv()
     for o in range(3):
-        left_total = left_total + xin[o].astype(jnp.float32)
-        right_total = right_total + yin[o].astype(jnp.float32)
+        left_total = left_total + xin[o]
+        right_total = right_total + yin[o]
     for q in range(4):
         stage[0, q] = left_total[64 * q : 64 * q + 64, :]
         stage[1, q] = right_total[64 * q : 64 * q + 64, :]
@@ -623,9 +623,9 @@
         scratch_shapes=[
             pltpu.VMEM((4, 2, 256, 256), f32),
             pltpu.VMEM((4, 2, 256, 256), f32),
-            pltpu.VMEM((2, 3, 256, 256), bf16),
-            pltpu.VMEM((3, 256, 256), bf16),
-            pltpu.VMEM((3, 256, 256), bf16),
+            pltpu.VMEM((2, 3, 256, 256), f32),
+            pltpu.VMEM((3, 256, 256), f32),
+            pltpu.VMEM((3, 256, 256), f32),
             pltpu.VMEM((2, 4, 64, 256), f32),
             pltpu.VMEM((3, 64, 256), f32),
             pltpu.VMEM((3, 64, 256), f32),

time: 228 us -> 229 us (level)
  no operation moved by 1% of the time
where the time goes in v8:
time: 229 us
  Pallas kernels  221 us (97%)
  local copies, waits for them, and re-layouts  4.25 us (2%)
  other arithmetic  2.76 us (1%)
    pallas_call x1, Pallas kernels, factor(): pl.pallas_call(factor_kernel, out_shape=(ups, ups, inverses, inverses), i...  89.7 us
    pallas_call x1, Pallas kernels, sketch_rows(): pl.pallas_call(lambda *refs: sketch_kernel(scale, total_rows, *refs), out...  68.9 us
    pallas_call x1, Pallas kernels, pcg(): pl.pallas_call(lambda *refs: pcg_kernel(total_rows, *refs), out_shape=jax...  62.7 us

profile of v8, /device:TPU:1, one launch (start us, length us, event | category | flops | bytes accessed | tf_op | source)
XLA Modules:
  0.0 229.1 jit_solution(12322274200595515577)
XLA Ops:
  0.0 0.7 add_select_fusion
  0.7 1.4 fusion.4.refs_4_
  2.1 0.7 fusion.8.refs_5_
  2.8 0.0 copy-start
  2.8 1.6 copy-done
  4.4 0.0 copy-start.1
  4.4 0.7 copy-done.1
  5.1 0.0 copy-start.2
  5.1 0.7 copy-done.2
  5.8 0.0 copy-start.3
  5.8 0.7 copy-done.3
  6.4 68.9 %sketch.1 = (bf16[2,4,4,64,1024]{4,3,2,1,0:T(8,128)(2,1)S(1)}, bf16[2,4,4,64,1024]{4,3,2,1,0:T(8,128)(2,1)S(1)}, f32[1,2048]{1,0:T(1,128)S(1)}, bf16[4,512,512]{2,1,0:T(8,128)(2,1)S(1)}) custom-call(bf16[2048,512]{1,0:T(8,128)(2,1)S(1)} %copy-done, f32[1,512]{1,0:T(1,128)S(1)} %bitcast.11, s32[1,2048]{1,0:T(1,128)S(1)} %bitcast.8, s32[1,2048]{1,0:T(1,128)S(1)} %bitcast.9, ...), custom_call_target="tpu_custom_call" | custom-call | tf_op jit(solution)/shard_map/sketch/pallas_call | solution.py:618
  75.4 0.0 copy-start.4
  75.4 89.7 %factor.1 = (bf16[6,512,512]{2,1,0:T(8,128)(2,1)S(1)}, bf16[6,512,512]{2,1,0:T(8,128)(2,1)S(1)}, bf16[4,512,512]{2,1,0:T(8,128)(2,1)S(1)}, bf16[4,512,512]{2,1,0:T(8,128)(2,1)S(1)}) custom-call(bf16[2048,1024]{1,0:T(8,128)(2,1)S(1)} %bitcast.13, bf16[2048,1024]{1,0:T(8,128)(2,1)S(1)} %bitcast.14), custom_call_target="tpu_custom_call" | custom-call | flops 60000002048 | bytes 18874368 | tf_op jit(solution)/shard_map/factor/pallas_call | solution.py:221
  165.8 0.0 copy-done.4
  165.8 62.7 %pcg.1 = f32[1,512]{1,0:T(1,128)S(1)} custom-call(bf16[4,512,512]{2,1,0:T(8,128)(2,1)S(1)} %get-tuple-element.13.refs_0_, f32[1,2048]{1,0:T(1,128)S(1)} %get-tuple-element.14.refs_1_, bf16[6,512,512]{2,1,0:T(8,128)(2,1)S(1)} %get-tuple-element.17.refs_2_, bf16[6,512,512]{2,1,0:T(8,128)(2,1)S(1)} %get-tuple-element.18.refs_3_, ...), custom_call_target="tpu_custom_call" | custom-call | tf_op jit(solution)/shard_map/pcg/pallas_call | solution.py:365
  228.5 0.6 copy.12
Async XLA Ops:
  2.8 1.6 copy-start
  4.4 0.7 copy-start.1
  5.1 0.7 copy-start.2
  5.8 0.7 copy-start.3
  75.4 90.4 %copy-start.4 = (f32[512]{0:T(512)S(1)}, f32[512]{0:T(512)}, u32[]{:S(2)}) copy-start(f32[512]{0:T(512)} %param.7) | copy-start | bytes 6148

commit v9 on v8

--- a/solution.py
+++ b/solution.py
@@ -190,17 +190,15 @@
                     up_hi[block, half, :] = ph
                     up_lo[block, half, :] = plo
 
-        def across(a, carry):
-            ra = pl.ds(pl.multiple_of(a * 512, 512), 512)
-
-            def along(b, carry):
-                cs = pl.ds(pl.multiple_of(b * 512, 512), 512)
-                gram[ra, cs] = gram[ra, cs] - lax.dot_general(trio_l[:, ra], trio_r[:, cs], TN, preferred_element_type=jnp.float32)
-                return carry
-
-            return lax.fori_loop(a, 4, along, carry)
-
-        lax.fori_loop((s + 1) // 2, 4, across, 0)
+        for a in range(4):
+
+            @pl.when(a >= (s + 1) // 2)
+            def _():
+                ra = slice(512 * a, 512 * a + 512)
+                for b in range(a, 4):
+                    cs = slice(512 * b, 512 * b + 512)
+                    gram[ra, cs] = gram[ra, cs] - lax.dot_general(trio_l[:, ra], trio_r[:, cs], TN, preferred_element_type=jnp.float32)
+
         return carry
 
     lax.fori_loop(0, 8, step, 0)

time: 229 us -> 227 us (level)
  Pallas kernels: 221 us -> 218 us
    pallas_call x1, Pallas kernels: 89.7 us -> 86.9 us  [factor(): pl.pallas_call(factor_kernel, out_shape=(ups, ups, inverses, inverses), i...]
where the time goes in v9:
time: 227 us; the launch traced here: 226 us
  Pallas kernels  218 us (96%)
  local copies, waits for them, and re-layouts  4.25 us (2%)
  other arithmetic  2.76 us (1%)
    pallas_call x1, Pallas kernels, factor(): pl.pallas_call(factor_kernel, out_shape=(ups, ups, inverses, inverses), i...  86.9 us
    pallas_call x1, Pallas kernels, sketch_rows(): pl.pallas_call(lambda *refs: sketch_kernel(scale, total_rows, *refs), out...  68.9 us
    pallas_call x1, Pallas kernels, pcg(): pl.pallas_call(lambda *refs: pcg_kernel(total_rows, *refs), out_shape=jax...  62.7 us

profile of v9, /device:TPU:1, one launch (start us, length us, event | category | flops | bytes accessed | tf_op | source)
XLA Modules:
  0.0 226.2 jit_solution(100840279295619127)
XLA Ops:
  0.0 0.7 add_select_fusion
  0.7 1.4 fusion.4.refs_4_
  2.1 0.7 fusion.8.refs_5_
  2.8 0.0 copy-start
  2.8 1.6 copy-done
  4.4 0.0 copy-start.1
  4.4 0.7 copy-done.1
  5.1 0.0 copy-start.2
  5.1 0.7 copy-done.2
  5.8 0.0 copy-start.3
  5.8 0.7 copy-done.3
  6.4 68.9 %sketch.1 = (bf16[2,4,4,64,1024]{4,3,2,1,0:T(8,128)(2,1)S(1)}, bf16[2,4,4,64,1024]{4,3,2,1,0:T(8,128)(2,1)S(1)}, f32[1,2048]{1,0:T(1,128)S(1)}, bf16[4,512,512]{2,1,0:T(8,128)(2,1)S(1)}) custom-call(bf16[2048,512]{1,0:T(8,128)(2,1)S(1)} %copy-done, f32[1,512]{1,0:T(1,128)S(1)} %bitcast.11, s32[1,2048]{1,0:T(1,128)S(1)} %bitcast.8, s32[1,2048]{1,0:T(1,128)S(1)} %bitcast.9, ...), custom_call_target="tpu_custom_call" | custom-call | tf_op jit(solution)/shard_map/sketch/pallas_call | solution.py:616
  75.4 0.0 copy-start.4
  75.4 86.9 %factor.1 = (bf16[6,512,512]{2,1,0:T(8,128)(2,1)S(1)}, bf16[6,512,512]{2,1,0:T(8,128)(2,1)S(1)}, bf16[4,512,512]{2,1,0:T(8,128)(2,1)S(1)}, bf16[4,512,512]{2,1,0:T(8,128)(2,1)S(1)}) custom-call(bf16[2048,1024]{1,0:T(8,128)(2,1)S(1)} %bitcast.13, bf16[2048,1024]{1,0:T(8,128)(2,1)S(1)} %bitcast.14), custom_call_target="tpu_custom_call" | custom-call | flops 60000002048 | bytes 18874368 | tf_op jit(solution)/shard_map/factor/pallas_call | solution.py:219
  162.9 0.0 copy-done.4
  162.9 62.7 %pcg.1 = f32[1,512]{1,0:T(1,128)S(1)} custom-call(bf16[4,512,512]{2,1,0:T(8,128)(2,1)S(1)} %get-tuple-element.13.refs_0_, f32[1,2048]{1,0:T(1,128)S(1)} %get-tuple-element.14.refs_1_, bf16[6,512,512]{2,1,0:T(8,128)(2,1)S(1)} %get-tuple-element.17.refs_2_, bf16[6,512,512]{2,1,0:T(8,128)(2,1)S(1)} %get-tuple-element.18.refs_3_, ...), custom_call_target="tpu_custom_call" | custom-call | tf_op jit(solution)/shard_map/pcg/pallas_call | solution.py:363
  225.6 0.6 copy.12
Async XLA Ops:
  2.8 1.6 copy-start
  4.4 0.7 copy-start.1
  5.1 0.7 copy-start.2
  5.8 0.7 copy-start.3
  75.4 87.5 %copy-start.4 = (f32[512]{0:T(512)S(1)}, f32[512]{0:T(512)}, u32[]{:S(2)}) copy-start(f32[512]{0:T(512)} %param.7) | copy-start | bytes 6148
